TPU v7x, 32 devices: a whole 2x2x4 slice. The times are simulated.
32 devices in a mesh: tm: 16 (over z, y, x), mp: 2 (over core).
Axes of the slice: x: 2, y: 2, z: 4, core: 2. Of those that a mesh axis runs over, the one named last changes fastest.
Arguments:
- frames: bfloat16 [5120, 1024], P('tm'), may hold values from -6 to 6
- valid: int32 [5120], P('tm'), may hold values from 0 to 1, as said below
- norm_gain: float32 [1024], replicated, may hold values from 0.1 to 1.9
- norm_bias: float32 [1024], replicated, may hold values from -3 to 3
- w_qkv: bfloat16 [3, 1024, 1024], P(None, None, 'mp'), may hold values from -8 to 8
- w_out: bfloat16 [1024, 1024], P(None, 'mp'), may hold values from -0.1875 to 0.1875
- conv_weight: float32 [9, 1024], P(None, 'mp'), may hold values from -2 to 2
- conv_scale: float32 [1024], P('mp'), may hold values from 0.5 to 2
- conv_shift: float32 [1024], P('mp'), may hold values from -3 to 3
Outputs:
- encoded: bfloat16 [5120, 1024], P('tm', 'mp')
Inputs may be any that keep to these rules, and one draw needn't show every extreme that they name: valid is 1 on a prefix of the frames and 0 on a final run of 1 to 128 frames.
All inputs are finite; a program needn't handle non-finite values.
Results may differ from a plain program's by a relative error of at most 0.0059.
Values may be sent and summed in bfloat16 or wider, within the bound.
No kernel may reach another device: no remote copies, remote signals or barrier semaphores. Data moves between devices by JAX's collectives and lax.ppermute only.
A program may use at most 64 MiB of HBM per device.

v0:
```python
import math

import jax
import jax.numpy as jnp
from jax import lax
from jax.sharding import PartitionSpec as P

HEAD_DIM = 128
CTX = 128
KERNEL = 9


def extended(value, sides, width):
    for axis, dim in sides:
        size, length = (lax.axis_size(axis), value.shape[dim])
        up = [(i, (i + 1) % size) for i in range(size - 1)]
        down = [(j, i) for i, j in up]
        last = lax.slice_in_dim(value, length - width, length, axis=dim)
        first = lax.slice_in_dim(value, 0, width, axis=dim)
        before = lax.ppermute(last, axis, up)
        after = lax.ppermute(first, axis, down)
        value = jnp.concatenate([before, value, after], axis=dim)
    return value


def layer_normed(frames, norm_gain, norm_bias):
    values = frames.astype(jnp.float32)
    center = values - jnp.mean(values, axis=-1, keepdims=True)
    spread = jnp.mean(center * center, axis=-1, keepdims=True)
    return (center * lax.rsqrt(spread + 1e-05) * norm_gain + norm_bias).astype(jnp.bfloat16)


def project(normed, matrix):
    return jnp.dot(normed, matrix, preferred_element_type=jnp.float32).astype(jnp.bfloat16)


def local(frames, valid, norm_gain, norm_bias, w_qkv, w_out, conv_weight, conv_scale, conv_shift):
    frame_count = frames.shape[0]
    local_width = w_qkv.shape[2]
    heads_here = local_width // HEAD_DIM
    out_width = w_out.shape[1]
    half_kernel = KERNEL // 2
    extra = 0
    reach = CTX + extra
    query_count = frame_count + 2 * extra
    normed = layer_normed(frames, norm_gain, norm_bias)
    queries = project(normed, w_qkv[0])
    valid_mark = valid.astype(jnp.bfloat16)
    pair_weight = jnp.concatenate([w_qkv[1], w_qkv[2]], axis=1)
    own_residual = lax.dynamic_slice_in_dim(frames, lax.axis_index("mp") * out_width, out_width, 1)
    pairs = project(normed, pair_weight)
    wide_sent, wide_valid = (
        extended(pairs, (("tm", 0),), reach),
        extended(valid_mark, (("tm", 0),), reach),
    )
    wide_count = frame_count + 2 * reach
    keys_all = wide_sent[:, :local_width].reshape(wide_count, heads_here, HEAD_DIM)
    values_all = wide_sent[:, local_width:].reshape(wide_count, heads_here, HEAD_DIM)
    query_heads = queries.reshape(query_count, heads_here, HEAD_DIM)
    scores = jnp.einsum(
        "thd,shd->hts", query_heads, keys_all, preferred_element_type=jnp.float32
    ) * (1.0 / math.sqrt(HEAD_DIM))
    offset = (
        jnp.arange(wide_count, dtype=jnp.int32)[None, :]
        - jnp.arange(query_count, dtype=jnp.int32)[:, None]
    )
    allowed = (offset >= 0) & (offset <= 2 * CTX) & (wide_valid[None, :] > 0.5)
    scores = jnp.where(allowed[None], scores, jnp.float32(-1e30))
    top = jnp.max(scores, axis=-1, keepdims=True)
    raised = jnp.exp(scores - top)
    weights = (raised / jnp.sum(raised, axis=-1, keepdims=True)).astype(jnp.bfloat16)
    attended = jnp.einsum("hts,shd->thd", weights, values_all, preferred_element_type=jnp.float32)
    attended = attended.astype(jnp.bfloat16).reshape(query_count, local_width)
    projected = jnp.dot(
        lax.all_gather(attended, "mp", axis=1, tiled=True),
        w_out,
        preferred_element_type=jnp.float32,
    )
    mixed_rows = (own_residual.astype(jnp.float32) + projected).astype(jnp.bfloat16)
    masked = mixed_rows * valid_mark[:, None]
    padded = extended(masked, (("tm", 0),), half_kernel)
    conv = jnp.zeros((frame_count, out_width), jnp.float32)
    for tap in range(KERNEL):
        conv = conv + padded[tap : tap + frame_count].astype(jnp.float32) * conv_weight[tap]
    return (mixed_rows.astype(jnp.float32) + jax.nn.silu(conv_scale * conv + conv_shift)).astype(
        jnp.bfloat16
    )


def solution(mesh):
    placed = (
        P("tm", None),
        P("tm"),
        P(),
        P(),
        P(None, None, "mp"),
        P(None, "mp"),
        P(None, "mp"),
        P("mp"),
        P("mp"),
    )
    return jax.shard_map(
        local, mesh=mesh, in_specs=placed, out_specs=P("tm", "mp"), check_vma=False
    )
```

profile of v0, /device:TPU:22, one launch (start us, length us, event | category | flops | bytes accessed | tf_op | source)
XLA Modules:
  0.0 42.2 jit_solution(17186530327096117569)
XLA Ops:
  0.0 0.0 copy-start
  0.0 1.4 %convert_reduce_fusion = f32[320]{0:T(512)S(1)} fusion(bf16[320,1024]{1,0:T(8,128)(2,1)} %param.9), kind=kLoop, calls=%fused_computation.14 | loop fusion | flops 655040 | bytes 656640 | tf_op jit(solution)/shard_map/reduce_sum | solution.py:28
  1.4 1.4 %fusion.15 = f32[320]{0:T(512)S(1)} fusion(bf16[320,1024]{1,0:T(8,128)(2,1)} %param.9, f32[320]{0:T(512)S(1)} %broadcast_multiply_fusion.1), kind=kLoop, calls=%fused_computation.18 | loop fusion | flops 1310400 | bytes 657920 | tf_op jit(solution)/shard_map/reduce_sum | solution.py:29
  2.8 0.0 copy-start.1
  2.8 0.0 copy-start.6
  2.8 0.0 copy-start.7
  2.8 1.7 %slice_bitcast_fusion.1 = (bf16[1024,512]{1,0:T(8,128)(2,1)S(1)}, bf16[1024,512]{1,0:T(8,128)(2,1)S(1)}) fusion(bf16[3,1024,512]{2,1,0:T(8,128)(2,1)} %param.13), kind=kLoop, calls=%fused_computation.32 | loop fusion | bytes 4194304 | tf_op jit(solution)/shard_map/squeeze | solution.py:49
  4.6 0.0 copy-done.1
  4.6 0.0 copy-done.6
  4.6 0.0 copy-done.7
  4.6 0.0 copy-start.5
  4.6 0.9 %fusion.12 = bf16[320,1024]{1,0:T(8,128)(2,1)S(1)} fusion(bf16[1024,512]{1,0:T(8,128)(2,1)S(1)} %get-tuple-element.6, bf16[1024,512]{1,0:T(8,128)(2,1)S(1)} %get-tuple-element.5, bf16[320,1024]{1,0:T(8,128)(2,1)S(1)} %copy-done.1, f32[1024]{0:T(1024)S(1)} %copy-done.6, f32[1024]{0:T(1024)S(1)} %copy-done.7, f32[320]{0:T(512)S(1)} %add_rsqrt_fusion, ...), kind=kOutput, calls=%fused_computation.17 | convolution fusion | flops 677576704 | bytes 3418624 | tf_op jit(solution)/shard_map/dot_general | solution.py:34
  5.5 0.7 %fusion.47 = (bf16[128,1024]{1,0:T(8,128)(2,1)}, bf16[128,1024]{1,0:T(8,128)(2,1)S(1)}) fusion(bf16[320,1024]{1,0:T(8,128)(2,1)S(1)} %fusion.12), kind=kLoop, calls=%fused_computation.72 | loop fusion | bytes 1048576 | tf_op jit(solution)/shard_map/slice | solution.py:18
  6.3 3.4 %collective-permute-start = (bf16[128,1024]{1,0:T(8,128)(2,1)}, bf16[128,1024]{1,0:T(8,128)(2,1)S(1)}, u32[]{:S(2)}, u32[]{:S(2)}) collective-permute-start(bf16[128,1024]{1,0:T(8,128)(2,1)} %get-tuple-element.9), channel_id=1, source_target_pairs={{0,2},{2,4},{4,6},{6,8},{8,10},{10,12},{12,14},{14,16},{16,18},{18... | collective-permute-start | bytes 786440 | tf_op jit(solution)/shard_map/ppermute | solution.py:20
  9.7 2.5 %collective-permute-start.1 = (bf16[128,1024]{1,0:T(8,128)(2,1)S(1)}, bf16[128,1024]{1,0:T(8,128)(2,1)S(1)}, u32[]{:S(2)}, u32[]{:S(2)}) collective-permute-start(bf16[128,1024]{1,0:T(8,128)(2,1)S(1)} %get-tuple-element.10), channel_id=1, source_target_pairs={{2,0},{4,2},{6,4},{8,6},{10,8},{12,10},{14,12},{16,14},{18,16},{20... | collective-permute-start | bytes 786440 | tf_op jit(solution)/shard_map/ppermute | solution.py:21
  12.1 0.0 copy-done.5
  12.1 0.1 fusion.50
  12.2 5.2 %collective-permute-start.2 = (bf16[128]{0:T(256)(128)(2,1)S(1)}, bf16[128]{0:T(256)(128)(2,1)S(1)}, u32[]{:S(2)}, u32[]{:S(2)}) collective-permute-start(bf16[128]{0:T(256)(128)(2,1)S(1)} %get-tuple-element.22), channel_id=1, source_target_pairs={{0,2},{2,4},{4,6},{6,8},{8,10},{10,12},{12,14},{14,16},{16,18},{18... | collective-permute-start | bytes 776 | tf_op jit(solution)/shard_map/ppermute | solution.py:20
  17.4 1.9 %collective-permute-start.3 = (bf16[128]{0:T(256)(128)(2,1)S(1)}, bf16[128]{0:T(256)(128)(2,1)S(1)}, u32[]{:S(2)}, u32[]{:S(2)}) collective-permute-start(bf16[128]{0:T(256)(128)(2,1)S(1)} %get-tuple-element.23), channel_id=1, source_target_pairs={{2,0},{4,2},{6,4},{8,6},{10,8},{12,10},{14,12},{16,14},{18,16},{20... | collective-permute-start | bytes 776 | tf_op jit(solution)/shard_map/ppermute | solution.py:21
  19.3 1.8 %fusion.22 = bf16[40,4,8,128]{3,2,1,0:T(8,128)(2,1)S(1)} fusion(bf16[3,1024,512]{2,1,0:T(8,128)(2,1)} %param.13, bf16[320,1024]{1,0:T(8,128)(2,1)S(1)} %copy-done.1, f32[1024]{0:T(1024)S(1)} %copy-done.6, f32[1024]{0:T(1024)S(1)} %copy-done.7, f32[320]{0:T(512)S(1)} %add_rsqrt_fusion, f32[320]{0:T(512)S(1)} %broadcast_multiply_fusion.1), kind=kOutput, calls=%fused_computation.27 | convolution fusion | flops 337674240 | bytes 2042368 | tf_op jit(solution)/shard_map/dot_general | solution.py:34
  21.1 0.9 %collective-permute-done.2 = bf16[128]{0:T(256)(128)(2,1)S(1)} collective-permute-done((bf16[128]{0:T(256)(128)(2,1)S(1)}, bf16[128]{0:T(256)(128)(2,1)S(1)}, u32[]{:S(2)}, u32[]{:S(2)}) %collective-permute-start.2) | collective-permute-done | bytes 288 | tf_op jit(solution)/shard_map/ppermute | solution.py:20
  22.0 2.6 %collective-permute-done.3 = bf16[128]{0:T(256)(128)(2,1)S(1)} collective-permute-done((bf16[128]{0:T(256)(128)(2,1)S(1)}, bf16[128]{0:T(256)(128)(2,1)S(1)}, u32[]{:S(2)}, u32[]{:S(2)}) %collective-permute-start.3) | collective-permute-done | bytes 288 | tf_op jit(solution)/shard_map/ppermute | solution.py:21
  24.7 0.1 maximum_compare_fusion
  24.7 0.1 fusion.28
  24.8 0.0 collective-permute-done
  24.8 0.0 collective-permute-done.1
  24.9 0.1 pad_maximum_fusion
  24.9 0.2 slice_bitcast_fusion.2
  25.2 0.6 %fusion.31 = f32[4,320,576]{2,1,0:T(8,128)S(1)} fusion(bf16[72,4,8,128]{3,2,1,0:T(8,128)(2,1)S(1)} %get-tuple-element.8, bf16[40,4,8,128]{3,2,1,0:T(8,128)(2,1)S(1)} %fusion.22), kind=kOutput, calls=%fused_computation.41 | convolution fusion | flops 188743680 | bytes 3866624 | tf_op jit(solution)/shard_map/thd,shd->hts/dot_general | solution.py:60
  25.8 1.7 %fusion.51 = (f32[4,320]{1,0:T(4,128)S(1)}, f32[4,320,576]{2,1,0:T(8,128)S(1)}) fusion(f32[4,320,576]{2,1,0:T(8,128)S(1)} %fusion.31, pred[320,576]{1,0:T(8,128)(4,1)S(1)} %fusion.28), kind=kOutput, calls=%fused_computation.76 | output fusion | flops 4424255 | bytes 6087680 | tf_op jit(solution)/shard_map/sub | solution.py:70
  27.5 0.7 %fusion.21 = bf16[4,40,8,128]{3,2,1,0:T(8,128)(2,1)S(1)} fusion(f32[4,320,576]{2,1,0:T(8,128)S(1)} %get-tuple-element.25, f32[4,320]{1,0:T(4,128)S(1)} %get-tuple-element.24, bf16[72,4,8,128]{3,2,1,0:T(8,128)(2,1)S(1)} %get-tuple-element.7), kind=kOutput, calls=%fused_computation.26 | convolution fusion | flops 190382080 | bytes 3871744 | tf_op jit(solution)/shard_map/hts,shd->thd/dot_general | solution.py:72
  28.1 0.0 copy-start.2
  28.2 0.0 copy-start.3
  28.2 0.0 copy-start.4
  28.2 0.1 copy.34
  28.2 2.3 %all_gather.3 = bf16[320,1024]{1,0:T(8,128)(2,1)S(1)} all-gather(bf16[320,512]{1,0:T(8,128)(2,1)S(1)} %bitcast.39), channel_id=1, replica_groups=mesh['tm'=16,'mp'=2] {'mp'}, dimensions={1}, use_global_device_ids=true | all-gather | bytes 983040 | tf_op jit(solution)/shard_map/all_gather | solution.py:75
  30.5 0.0 copy-done
  30.5 0.5 %broadcast_multiply_fusion = (bf16[320,512]{1,0:T(8,128)(2,1)S(1)}, bf16[320,512]{1,0:T(8,128)(2,1)S(1)}) fusion(bf16[320]{0:T(512)(128)(2,1)S(1)} %convert_element_type.67, bf16[320,1024]{1,0:T(8,128)(2,1)S(1)} %all_gather.3, bf16[1024,512]{1,0:T(8,128)(2,1)S(1)} %copy-done, bf16[320,1024]{1,0:T(8,128)(2,1)S(1)} %copy-done.1, s32[]{:T(128)S(6)} %select_n.7), kind=kOutput, calls=%fused_computation.65 | convolution fusion | flops 336691200 | bytes 2687620 | tf_op jit(solution)/shard_map/dot_general | solution.py:74
  31.0 2.2 %collective-permute-start.4 = (bf16[4,512]{1,0:T(4,128)(2,1)S(1)}, bf16[4,512]{1,0:T(4,128)(2,1)S(1)}, u32[]{:S(2)}, u32[]{:S(2)}) collective-permute-start(bf16[4,512]{1,0:T(4,128)(2,1)S(1)} %get-tuple-element.11), channel_id=1, source_target_pairs={{0,2},{2,4},{4,6},{6,8},{8,10},{10,12},{12,14},{14,16},{16,18},{18... | collective-permute-start | bytes 12296 | tf_op jit(solution)/shard_map/ppermute | solution.py:20
  33.3 3.6 %collective-permute-start.5 = (bf16[4,512]{1,0:T(4,128)(2,1)S(1)}, bf16[4,512]{1,0:T(4,128)(2,1)S(1)}, u32[]{:S(2)}, u32[]{:S(2)}) collective-permute-start(bf16[4,512]{1,0:T(4,128)(2,1)S(1)} %get-tuple-element.12), channel_id=1, source_target_pairs={{2,0},{4,2},{6,4},{8,6},{10,8},{12,10},{14,12},{16,14},{18,16},{20... | collective-permute-start | bytes 12296 | tf_op jit(solution)/shard_map/ppermute | solution.py:21
  36.9 0.0 copy-done.2
  36.9 0.0 collective-permute-done.4
  37.0 3.6 %collective-permute-done.5 = bf16[4,512]{1,0:T(4,128)(2,1)S(1)} collective-permute-done((bf16[4,512]{1,0:T(4,128)(2,1)S(1)}, bf16[4,512]{1,0:T(4,128)(2,1)S(1)}, u32[]{:S(2)}, u32[]{:S(2)}) %collective-permute-start.5) | collective-permute-done | bytes 4128 | tf_op jit(solution)/shard_map/ppermute | solution.py:21
  40.6 0.0 copy-done.3
  40.6 0.0 copy-done.4
  40.6 1.6 %add_convert_fusion = bf16[320,512]{1,0:T(8,128)(2,1)} fusion(bf16[320,512]{1,0:T(8,128)(2,1)S(1)} %get-tuple-element.26, bf16[320,512]{1,0:T(8,128)(2,1)S(1)} %get-tuple-element.27, bf16[4,512]{1,0:T(4,128)(2,1)S(1)} %collective-permute-done.5, bf16[4,512]{1,0:T(4,128)(2,1)S(1)} %collective-permute-done.4, f32[512]{0:T(512)S(1)} %copy-done.3, ...), kind=kLoop, calls=%fused_computation.38 | loop fusion | flops 9666560 | bytes 1013760 | tf_op jit(solution)/shard_map/convert_element_type | solution.py:85
  (5 shorter events, 0.0 us)
Async XLA Ops:
  0.0 30.5 %copy-start = (bf16[1024,512]{1,0:T(8,128)(2,1)S(1)}, bf16[1024,512]{1,0:T(8,128)(2,1)}, u32[]{:S(2)}) copy-start(bf16[1024,512]{1,0:T(8,128)(2,1)} %param.14) | copy-start | bytes 3145732
  2.8 1.8 %copy-start.1 = (bf16[320,1024]{1,0:T(8,128)(2,1)S(1)}, bf16[320,1024]{1,0:T(8,128)(2,1)}, u32[]{:S(2)}) copy-start(bf16[320,1024]{1,0:T(8,128)(2,1)} %param.9) | copy-start | bytes 1966084
  2.8 1.8 %copy-start.6 = (f32[1024]{0:T(1024)S(1)}, f32[1024]{0:T(1024)}, u32[]{:S(2)}) copy-start(f32[1024]{0:T(1024)} %param.12) | copy-start | bytes 12292
  2.8 1.8 %copy-start.7 = (f32[1024]{0:T(1024)S(1)}, f32[1024]{0:T(1024)}, u32[]{:S(2)}) copy-start(f32[1024]{0:T(1024)} %param.11) | copy-start | bytes 12292
  4.6 7.5 %copy-start.5 = (s32[320]{0:T(512)S(1)}, s32[320]{0:T(512)}, u32[]{:S(2)}) copy-start(s32[320]{0:T(512)} %param.10) | copy-start | bytes 3844
  6.3 18.6 %collective-permute-start = (bf16[128,1024]{1,0:T(8,128)(2,1)}, bf16[128,1024]{1,0:T(8,128)(2,1)S(1)}, u32[]{:S(2)}, u32[]{:S(2)}) collective-permute-start(bf16[128,1024]{1,0:T(8,128)(2,1)} %get-tuple-element.9), channel_id=1, source_target_pairs={{0,2},{2,4},{4,6},{6,8},{8,10},{10,12},{12,14},{14,16},{16,18},{18... | collective-permute-start | bytes 786440 | tf_op jit(solution)/shard_map/ppermute | solution.py:20
  9.7 15.2 %collective-permute-start.1 = (bf16[128,1024]{1,0:T(8,128)(2,1)S(1)}, bf16[128,1024]{1,0:T(8,128)(2,1)S(1)}, u32[]{:S(2)}, u32[]{:S(2)}) collective-permute-start(bf16[128,1024]{1,0:T(8,128)(2,1)S(1)} %get-tuple-element.10), channel_id=1, source_target_pairs={{2,0},{4,2},{6,4},{8,6},{10,8},{12,10},{14,12},{16,14},{18,16},{20... | collective-permute-start | bytes 786440 | tf_op jit(solution)/shard_map/ppermute | solution.py:21
  12.2 9.8 %collective-permute-start.2 = (bf16[128]{0:T(256)(128)(2,1)S(1)}, bf16[128]{0:T(256)(128)(2,1)S(1)}, u32[]{:S(2)}, u32[]{:S(2)}) collective-permute-start(bf16[128]{0:T(256)(128)(2,1)S(1)} %get-tuple-element.22), channel_id=1, source_target_pairs={{0,2},{2,4},{4,6},{6,8},{8,10},{10,12},{12,14},{14,16},{16,18},{18... | collective-permute-start | bytes 776 | tf_op jit(solution)/shard_map/ppermute | solution.py:20
  17.4 7.3 %collective-permute-start.3 = (bf16[128]{0:T(256)(128)(2,1)S(1)}, bf16[128]{0:T(256)(128)(2,1)S(1)}, u32[]{:S(2)}, u32[]{:S(2)}) collective-permute-start(bf16[128]{0:T(256)(128)(2,1)S(1)} %get-tuple-element.23), channel_id=1, source_target_pairs={{2,0},{4,2},{6,4},{8,6},{10,8},{12,10},{14,12},{16,14},{18,16},{20... | collective-permute-start | bytes 776 | tf_op jit(solution)/shard_map/ppermute | solution.py:21
  28.1 8.8 %copy-start.2 = (f32[9,512]{1,0:T(8,128)S(1)}, f32[9,512]{1,0:T(8,128)}, u32[]{:S(2)}) copy-start(f32[9,512]{1,0:T(8,128)} %param.15) | copy-start | bytes 55300
  28.2 12.4 %copy-start.3 = (f32[512]{0:T(512)S(1)}, f32[512]{0:T(512)}, u32[]{:S(2)}) copy-start(f32[512]{0:T(512)} %param.17) | copy-start | bytes 6148
  28.2 12.4 %copy-start.4 = (f32[512]{0:T(512)S(1)}, f32[512]{0:T(512)}, u32[]{:S(2)}) copy-start(f32[512]{0:T(512)} %param.16) | copy-start | bytes 6148
  31.0 5.9 %collective-permute-start.4 = (bf16[4,512]{1,0:T(4,128)(2,1)S(1)}, bf16[4,512]{1,0:T(4,128)(2,1)S(1)}, u32[]{:S(2)}, u32[]{:S(2)}) collective-permute-start(bf16[4,512]{1,0:T(4,128)(2,1)S(1)} %get-tuple-element.11), channel_id=1, source_target_pairs={{0,2},{2,4},{4,6},{6,8},{8,10},{10,12},{12,14},{14,16},{16,18},{18... | collective-permute-start | bytes 12296 | tf_op jit(solution)/shard_map/ppermute | solution.py:20
  33.3 7.3 %collective-permute-start.5 = (bf16[4,512]{1,0:T(4,128)(2,1)S(1)}, bf16[4,512]{1,0:T(4,128)(2,1)S(1)}, u32[]{:S(2)}, u32[]{:S(2)}) collective-permute-start(bf16[4,512]{1,0:T(4,128)(2,1)S(1)} %get-tuple-element.12), channel_id=1, source_target_pairs={{2,0},{4,2},{6,4},{8,6},{10,8},{12,10},{14,12},{16,14},{18,16},{20... | collective-permute-start | bytes 12296 | tf_op jit(solution)/shard_map/ppermute | solution.py:21
where the time goes:
time: 42.6 us; the launch traced here: 42.2 us
  starting transfers between devices  18.8 us (44%)
  waiting for transfers between devices  7.15 us (17%)
  other arithmetic  6.4 us (15%)
  matrix products  4.47 us (10%)
  local copies, waits for them, and re-layouts  2.89 us (7%)
  blocking collectives  2.28 us (5%)
    ppermute x3, starting transfers between devices, extended(): before = lax.ppermute(last, axis, up)  10.7 us
    ppermute x3, starting transfers between devices, extended(): after = lax.ppermute(first, axis, down)  8.02 us
    ppermute x3, waiting for transfers between devices, extended(): after = lax.ppermute(first, axis, down)  6.24 us
    dot_general x2, matrix products, project(): jnp.dot(normed, matrix, preferred_element_type=jnp.float32)  2.7 us
    all_gather x1, blocking collectives, local(): lax.all_gather(attended, 'mp', axis=1, tiled=True)  2.28 us
    squeeze x1, local copies, waits for them, and re-layouts, local(): pair_weight = jnp.concatenate([w_qkv[1], w_qkv[2]], axis=1)  1.74 us
    sub x1, other arithmetic, local(): raised = jnp.exp(scores - top)  1.7 us
    convert_element_type x1, other arithmetic, local(): (mixed_rows.astype(jnp.float32) + jax.nn.silu(conv_scale * conv + conv_sh...  1.64 us
  transfers between devices with their start and end apart: 6, of which 3 were waited for; matrix products, arithmetic and copies ran while one was open for 5% of the time, Pallas kernels for 0%

commit v1 on v0

v1 whole, which is shorter than its diff:
```python
import math

import jax
import jax.numpy as jnp
from jax import lax
from jax.experimental import pallas as pl
from jax.experimental.pallas import tpu as pltpu
from jax.sharding import PartitionSpec as P

HEAD_DIM = 128
CTX = 128
KERNEL = 9
EXT = 8
HALO = CTX + EXT
NEG = -1e30
SCALE = math.log2(math.e) / math.sqrt(HEAD_DIM)
VMEM = pl.BlockSpec(memory_space=pltpu.VMEM)


def layer_normed(values, gain, bias):
    center = values - jnp.mean(values, axis=-1, keepdims=True)
    spread = jnp.mean(center * center, axis=-1, keepdims=True)
    return center * lax.rsqrt(spread + 1e-05) * gain + bias


def dot(a, b):
    return jnp.dot(a, b, preferred_element_type=jnp.float32)


def dot_t(a, b):
    return lax.dot_general(a, b, (((1,), (1,)), ((), ())), preferred_element_type=jnp.float32)


def positions(shape, dim, start):
    return lax.broadcasted_iota(jnp.int32, shape, dim) + start


def own_kernel(
    frames, valid, gain, bias, w, q_out, k_out, v_out, top_out, total_out, acc_out, normed
):
    rows = frames.shape[0]
    p = lax.axis_index("mp")
    keys, queries = k_out.shape[0], q_out.shape[0]
    key_at = p * (rows - keys)
    query_at = p * (rows - queries)
    count = jnp.sum(valid[...])
    values = frames[pl.ds(pl.multiple_of(key_at, 8), keys), :].astype(jnp.float32)
    normed[...] = layer_normed(values, gain[...], bias[...]).astype(jnp.bfloat16)
    k_out[...] = dot(normed[...], w[1]).astype(jnp.bfloat16)
    v_out[...] = dot(normed[...], w[2]).astype(jnp.bfloat16)
    picked = normed[pl.ds(pl.multiple_of(p * (keys - queries), 16), queries), :]
    q_out[...] = dot(picked, w[0]).astype(jnp.bfloat16)
    key_pos = positions((queries, keys), 1, key_at)
    query_pos = positions((queries, keys), 0, query_at)
    allowed = (jnp.abs(key_pos - query_pos) <= CTX) & (key_pos < count)
    for head in range(q_out.shape[1] // HEAD_DIM):
        at = slice(head * HEAD_DIM, (head + 1) * HEAD_DIM)
        scores = dot_t(q_out[:, at], k_out[:, at]) * SCALE
        scores = jnp.where(allowed, scores, NEG)
        top = jnp.max(scores, axis=-1, keepdims=True)
        raised = jnp.exp2(scores - top)
        total = jnp.sum(raised, axis=-1, keepdims=True)
        top_out[head] = jnp.broadcast_to(top, (queries, HEAD_DIM))
        total_out[head] = jnp.broadcast_to(total, (queries, HEAD_DIM))
        acc_out[:, at] = dot(raised.astype(jnp.bfloat16), v_out[:, at])


def halo_kernel(halo, frames, gain, bias, *refs):
    (w_a, wo_a, q_a, k_a, v_a, top_a, total_a, acc_a) = refs[:8]
    (w_b, wo_b, q_b, k_b, v_b, top_b, total_b, acc_b) = refs[8:16]
    keep, send, normed, far_normed, q_halo, att = refs[16:]
    p = lax.axis_index("mp")
    last = lax.axis_size("tm") - 1
    tm = lax.axis_index("tm")
    rows, queries, keys = frames.shape[0], q_a.shape[0], k_a.shape[0]
    width = q_a.shape[1]
    present = jnp.where(p == 0, tm > 0, tm < last)
    near = halo[pl.ds(pl.multiple_of(EXT * (1 - p), 8), CTX), :].astype(jnp.float32)
    far = halo[pl.ds(pl.multiple_of(CTX * p, 8), EXT), :].astype(jnp.float32)
    values = layer_normed(jnp.concatenate([near, far], axis=0), gain[...], bias[...])
    far_normed[...] = values
    normed[...] = values.astype(jnp.bfloat16)
    ext_normed = far_normed[pl.ds(pl.multiple_of((CTX - EXT) * (1 - p), 8), EXT), :]
    ext_normed = ext_normed.astype(jnp.bfloat16)
    near_at = jnp.where(p == 0, -CTX, rows)
    far_at = jnp.where(p == 0, -HALO, rows + CTX)
    ext_at = jnp.where(p == 0, -EXT, rows)
    touched = p * (queries - CTX)
    query_pos = positions((CTX, CTX), 0, p * (rows - CTX))
    near_pos = positions((CTX, CTX), 1, near_at)
    allowed = (jnp.abs(near_pos - query_pos) <= CTX) & present
    own_at = p * (keys - CTX)
    ext_own = jnp.abs(positions((EXT, CTX), 1, p * (rows - CTX)) - positions((EXT, CTX), 0, ext_at)) <= CTX
    ext_near = jnp.abs(positions((EXT, CTX), 1, near_at) - positions((EXT, CTX), 0, ext_at)) <= CTX
    ext_far = jnp.abs(positions((EXT, EXT), 1, far_at) - positions((EXT, EXT), 0, ext_at)) <= CTX
    for side, (w, q, k, v, top_own, total_own, acc_own) in enumerate(
        ((w_a, q_a, k_a, v_a, top_a, total_a, acc_a), (w_b, q_b, k_b, v_b, top_b, total_b, acc_b))
    ):
        k_halo = dot(normed[...], w[1])
        v_halo = dot(normed[...], w[2])
        q_ext = dot(ext_normed, w[0])
        for head in range(width // HEAD_DIM):
            at = slice(head * HEAD_DIM, (head + 1) * HEAD_DIM)
            to = slice(side * width + at.start, side * width + at.stop)
            k_near = k_halo[:CTX, at].astype(jnp.bfloat16)
            v_near = v_halo[:CTX, at].astype(jnp.bfloat16)
            k_far = k_halo[CTX:, at].astype(jnp.bfloat16)
            v_far = v_halo[CTX:, at].astype(jnp.bfloat16)
            part = pl.ds(pl.multiple_of(touched, 8), CTX)
            scores = dot_t(q[part, at], k_near) * SCALE
            scores = jnp.where(allowed, scores, NEG)
            before = top_own[head, part, :]
            top = jnp.maximum(before, jnp.max(scores, axis=-1, keepdims=True))
            raised = jnp.exp2(scores - top)
            faded = jnp.exp2(before - top)
            total = total_own[head, part, :] * faded + jnp.sum(raised, axis=-1, keepdims=True)
            acc = acc_own[part, at] * faded + dot(raised.astype(jnp.bfloat16), v_near)
            att[:queries, to] = acc_own[:, at] / total_own[head]
            att[part, to] = acc / total
            q_head = q_ext[:, at].astype(jnp.bfloat16)
            own = pl.ds(pl.multiple_of(own_at, 8), CTX)
            s_own = jnp.where(ext_own, dot_t(q_head, k[own, at]) * SCALE, NEG)
            s_near = jnp.where(ext_near, dot_t(q_head, k_near) * SCALE, NEG)
            s_far = jnp.where(ext_far, dot_t(q_head, k_far) * SCALE, NEG)
            top = jnp.maximum(
                jnp.maximum(
                    jnp.max(s_own, axis=-1, keepdims=True), jnp.max(s_near, axis=-1, keepdims=True)
                ),
                jnp.max(s_far, axis=-1, keepdims=True),
            )
            r_own, r_near, r_far = jnp.exp2(s_own - top), jnp.exp2(s_near - top), jnp.exp2(s_far - top)
            total = (
                jnp.sum(r_own, axis=-1, keepdims=True)
                + jnp.sum(r_near, axis=-1, keepdims=True)
                + jnp.sum(r_far, axis=-1, keepdims=True)
            )
            acc = (
                dot(r_own.astype(jnp.bfloat16), v[own, at])
                + dot(r_near.astype(jnp.bfloat16), v_near)
                + dot(r_far.astype(jnp.bfloat16), v_far)
            )
            att[queries:, to] = acc / total
    attended = att[...].astype(jnp.bfloat16)
    here = pl.ds(pl.multiple_of(p * width, width), width)
    there = pl.ds(pl.multiple_of((1 - p) * width, width), width)
    own_rows = pl.ds(pl.multiple_of(p * (rows - queries), 8), queries)
    ext_rows = pl.ds(pl.multiple_of(CTX * (1 - p), 8), EXT)
    for wo, columns, out in ((wo_b, there, send), (wo_a, here, keep)):
        projected = dot(attended[:, :width], wo[here, :]) + dot(attended[:, width:], wo[there, :])
        out[:queries] = (frames[own_rows, columns].astype(jnp.float32) + projected[:queries]).astype(
            jnp.bfloat16
        )
        out[queries:] = (halo[ext_rows, columns].astype(jnp.float32) + projected[queries:]).astype(
            jnp.bfloat16
        )


def conv_kernel(keep, got, valid, weight, scale, shift, out, plain, masked):
    p = lax.axis_index("mp")
    tm = lax.axis_index("tm")
    last = lax.axis_size("tm") - 1
    rows = out.shape[0]
    half = rows // 2
    queries = keep.shape[0] - EXT
    count = jnp.sum(valid[...])

    def place(block, core):
        start = pl.ds(pl.multiple_of(core * (queries - half), 8), half)
        plain[pl.ds(pl.multiple_of(EXT + core * half, 8), half), :] = block[start, :].astype(
            jnp.float32
        )
        edge = block[queries:, :].astype(jnp.float32)
        inside = jnp.where(core == 0, tm > 0, tm < last)
        masked[pl.ds(pl.multiple_of(core * (EXT + rows), 8), EXT), :] = jnp.where(inside, edge, 0.0)

    place(keep, p)
    place(got, 1 - p)
    step = 32
    for at in range(0, rows, step):
        values = plain[EXT + at : EXT + at + step, :]
        row = positions(values.shape, 0, at)
        masked[EXT + at : EXT + at + step, :] = jnp.where(row < count, values, 0.0)
    for column in range(0, out.shape[1], 128):
        lanes = slice(column, column + 128)
        for at in range(0, rows, step):
            conv = jnp.zeros((step, 128), jnp.float32)
            for tap in range(KERNEL):
                begin = EXT - KERNEL // 2 + at + tap
                conv = conv + masked[begin : begin + step, lanes] * weight[tap : tap + 1, lanes]
            v = scale[:, lanes] * conv + shift[:, lanes]
            out[at : at + step, lanes] = (
                plain[EXT + at : EXT + at + step, lanes] + v / (1.0 + jnp.exp(-v))
            ).astype(jnp.bfloat16)


def local(frames, valid, norm_gain, norm_bias, w_qkv, w_out, conv_weight, conv_scale, conv_shift):
    rows, model = frames.shape
    width = w_qkv.shape[2]
    heads = width // HEAD_DIM
    count = lax.axis_size("tm")
    mp = lax.axis_index("mp")
    half = rows // 2
    queries = half + EXT
    keys = half + EXT + CTX
    assert rows >= HALO + CTX and rows % 16 == 0
    pairs = []
    for i in range(count - 1):
        pairs += [(2 * i, 2 * (i + 1)), (2 * (i + 1) + 1, 2 * i + 1)]
    other = [(0, 1), (1, 0)]
    sent = lax.dynamic_slice_in_dim(frames, (1 - mp) * (rows - HALO), HALO, 0)
    halo = lax.ppermute(sent, ("tm", "mp"), pairs)
    w_other = lax.ppermute(w_qkv, "mp", other)
    wo_other = lax.ppermute(w_out, "mp", other)
    valid = valid.reshape(1, rows)
    gain, bias = norm_gain.reshape(1, model), norm_bias.reshape(1, model)

    def own(w):
        f32, bf16 = jnp.float32, jnp.bfloat16
        return pl.pallas_call(
            own_kernel,
            out_shape=(
                jax.ShapeDtypeStruct((queries, width), bf16),
                jax.ShapeDtypeStruct((keys, width), bf16),
                jax.ShapeDtypeStruct((keys, width), bf16),
                jax.ShapeDtypeStruct((heads, queries, HEAD_DIM), f32),
                jax.ShapeDtypeStruct((heads, queries, HEAD_DIM), f32),
                jax.ShapeDtypeStruct((queries, width), f32),
            ),
            in_specs=[VMEM] * 5,
            out_specs=(VMEM,) * 6,
            scratch_shapes=[pltpu.VMEM((keys, model), bf16)],
            compiler_params=pltpu.CompilerParams(vmem_limit_bytes=20 << 20),
            cost_estimate=pl.CostEstimate(
                flops=2_000_000_000, bytes_accessed=4_000_000, transcendentals=300_000
            ),
            name="own",
        )(frames, valid, gain, bias, w)

    mine = own(w_qkv)
    theirs = own(w_other)
    keep, send = pl.pallas_call(
        halo_kernel,
        out_shape=(jax.ShapeDtypeStruct((queries + EXT, width), jnp.bfloat16),) * 2,
        in_specs=[VMEM] * 20,
        out_specs=(VMEM,) * 2,
        scratch_shapes=[
            pltpu.VMEM((HALO, model), jnp.bfloat16),
            pltpu.VMEM((HALO, model), jnp.float32),
            pltpu.VMEM((EXT, model), jnp.float32),
            pltpu.VMEM((queries + EXT, 2 * width), jnp.float32),
        ],
        compiler_params=pltpu.CompilerParams(vmem_limit_bytes=20 << 20),
        cost_estimate=pl.CostEstimate(
            flops=1_500_000_000, bytes_accessed=10_000_000, transcendentals=300_000
        ),
        name="halo",
    )(halo, frames, gain, bias, w_qkv, w_out, *mine, w_other, wo_other, *theirs)
    got = lax.ppermute(send, "mp", other)
    return pl.pallas_call(
        conv_kernel,
        out_shape=jax.ShapeDtypeStruct((rows, width), jnp.bfloat16),
        in_specs=[VMEM] * 6,
        out_specs=VMEM,
        scratch_shapes=[pltpu.VMEM((rows + 2 * EXT, width), jnp.float32)] * 2,
        compiler_params=pltpu.CompilerParams(vmem_limit_bytes=20 << 20),
        name="conv",
    )(keep, got, valid, conv_weight, conv_scale.reshape(1, width), conv_shift.reshape(1, width))


def solution(mesh):
    placed = (
        P("tm", None),
        P("tm"),
        P(),
        P(),
        P(None, None, "mp"),
        P(None, "mp"),
        P(None, "mp"),
        P("mp"),
        P("mp"),
    )
    return jax.shard_map(
        local, mesh=mesh, in_specs=placed, out_specs=P("tm", "mp"), check_vma=False
    )
```

time: 42.6 us -> 26 us (0.61)
  the two profiles are of different devices: /device:TPU:22 before, /device:TPU:0 now
where the time goes in v1:
time: 26 us; the launch traced here: 25.7 us
  Pallas kernels  12.6 us (48%)
  local copies, waits for them, and re-layouts  6.05 us (23%)
  starting transfers between devices  5.47 us (21%)
  waiting for transfers between devices  1.41 us (5%)
    pallas_call x1, Pallas kernels, local(): pl.pallas_call(halo_kernel, out_shape=(jax.ShapeDtypeStruct((queries + EX...  5.7 us
    pallas_call x2, Pallas kernels, own(): pl.pallas_call(own_kernel, out_shape=(jax.ShapeDtypeStruct((queries, widt...  4.9 us
    ppermute x1, starting transfers between devices, local(): halo = lax.ppermute(sent, ('tm', 'mp'), pairs)  4.89 us
    unnamed x22, local copies, waits for them, and re-layouts  4.39 us
    pallas_call x1, Pallas kernels, local(): pl.pallas_call(conv_kernel, out_shape=jax.ShapeDtypeStruct((rows, width),...  1.97 us
    ppermute x1, waiting for transfers between devices, local(): got = lax.ppermute(send, 'mp', other)  1.4 us
    dynamic_slice x1, local copies, waits for them, and re-layouts, local(): sent = lax.dynamic_slice_in_dim(frames, (1 - mp) * (rows - HALO), HALO, 0)  0.97 us
    reshape x1, local copies, waits for them, and re-layouts, local(): valid = valid.reshape(1, rows)  0.69 us
  transfers between devices with their start and end apart: 4, of which 1 were waited for; matrix products, arithmetic and copies ran while one was open for 6% of the time, Pallas kernels for 19%

profile of v1, /device:TPU:0, one launch (start us, length us, event | category | flops | bytes accessed | tf_op | source)
XLA Modules:
  0.0 25.7 jit_solution(11575318321574742340)
XLA Ops:
  0.0 0.5 %collective-permute-start.1 = (bf16[3,1024,512]{2,1,0:T(8,128)(2,1)}, bf16[3,1024,512]{2,1,0:T(8,128)(2,1)S(1)}, u32[]{:S(2)}, u32[]{:S(2)}) collective-permute-start(bf16[3,1024,512]{2,1,0:T(8,128)(2,1)} %refs_0_.1), channel_id=1, source_target_pairs={{0,1},{1,0},{2,3},{3,2},{4,5},{5,4},{6,7},{7,6},{8,9},{9,8},{10,11... | collective-permute-start | bytes 9437192 | tf_op jit(solution)/shard_map/ppermute | solution.py:212
  0.5 0.0 collective-permute-start.2
  0.5 1.0 %constant_dynamic-slice_fusion = bf16[136,1024]{1,0:T(8,128)(2,1)S(1)} fusion(bf16[320,1024]{1,0:T(8,128)(2,1)} %frames.5, s32[]{:T(128)S(6)} %select_n.3), kind=kLoop, calls=%fused_computation | loop fusion | bytes 557060 | tf_op jit(solution)/shard_map/dynamic_slice | solution.py:210
  1.5 4.9 %collective-permute-start = (bf16[136,1024]{1,0:T(8,128)(2,1)S(1)}, bf16[136,1024]{1,0:T(8,128)(2,1)S(1)}, u32[]{:S(2)}, u32[]{:S(2)}) collective-permute-start(bf16[136,1024]{1,0:T(8,128)(2,1)S(1)} %constant_dynamic-slice_fusion), channel_id=1, source_target_pairs={{0,2},{3,1},{2,4},{5,3},{4,6},{7,5},{6,8},{9,7},{8,10},{11,9},{10,... | collective-permute-start | bytes 835592 | tf_op jit(solution)/shard_map/ppermute | solution.py:211
  6.4 0.7 %reshape.17.valid = s32[1,320]{1,0:T(1,128)S(1)} reshape(s32[320]{0:T(512)} %param.10) | data formatting | bytes 2560 | tf_op jit(solution)/shard_map/reshape | solution.py:214
  7.1 0.0 copy-start
  7.1 1.9 %copy-done = bf16[3,1024,512]{2,1,0:T(8,128)(2,1)S(1)} copy-done((bf16[3,1024,512]{2,1,0:T(8,128)(2,1)S(1)}, bf16[3,1024,512]{2,1,0:T(8,128)(2,1)}, u32[]{:S(2)}) %copy-start) | copy-done | bytes 3145752
  9.0 0.0 copy-start.2
  9.0 1.1 %copy-done.2 = bf16[320,1024]{1,0:T(8,128)(2,1)S(1)} copy-done((bf16[320,1024]{1,0:T(8,128)(2,1)S(1)}, bf16[320,1024]{1,0:T(8,128)(2,1)}, u32[]{:S(2)}) %copy-start.2) | copy-done | bytes 655384
  10.0 0.0 copy-start.6
  10.1 0.7 %copy-done.6 = f32[1024]{0:T(1024)S(1)} copy-done((f32[1024]{0:T(1024)S(1)}, f32[1024]{0:T(1024)}, u32[]{:S(2)}) %copy-start.6) | copy-done | bytes 4120
  10.7 0.0 copy-start.7
  10.7 0.7 %copy-done.7 = f32[1024]{0:T(1024)S(1)} copy-done((f32[1024]{0:T(1024)S(1)}, f32[1024]{0:T(1024)}, u32[]{:S(2)}) %copy-start.7) | copy-done | bytes 4120
  11.4 0.0 copy-start.8
  11.4 2.5 %own.2 = (bf16[168,512]{1,0:T(8,128)(2,1)S(1)}, bf16[296,512]{1,0:T(8,128)(2,1)S(1)}, bf16[296,512]{1,0:T(8,128)(2,1)S(1)}, f32[4,168,128]{2,1,0:T(8,128)S(1)}, ...) custom-call(bf16[320,1024]{1,0:T(8,128)(2,1)S(1)} %copy-done.2, s32[1,320]{1,0:T(1,128)S(1)} %reshape.17.valid, ...), custom_call_target="tpu_custom_call" | custom-call | flops 2000000000 | bytes 4000000 | tf_op jit(solution)/shard_map/own/pallas_call | solution.py:219
  13.9 0.0 copy-start.1
  13.9 0.0 copy-start.3
  13.9 0.0 copy-start.4
  13.9 0.0 collective-permute-done.1.w.refs_8_
  13.9 0.0 copy-done.8
  13.9 2.5 %own.3 = (bf16[168,512]{1,0:T(8,128)(2,1)S(1)}, bf16[296,512]{1,0:T(8,128)(2,1)S(1)}, bf16[296,512]{1,0:T(8,128)(2,1)S(1)}, f32[4,168,128]{2,1,0:T(8,128)S(1)}, ...) custom-call(bf16[320,1024]{1,0:T(8,128)(2,1)S(1)} %copy-done.2, s32[1,320]{1,0:T(1,128)S(1)} %reshape.17.valid, ...), custom_call_target="tpu_custom_call" | custom-call | flops 2000000000 | bytes 4000000 | tf_op jit(solution)/shard_map/own/pallas_call | solution.py:219
  16.4 0.0 collective-permute-done.halo
  16.4 0.0 collective-permute-done.2.refs_9_
  16.4 0.0 copy-done.1
  16.4 0.0 copy-done.3
  16.4 0.0 copy-done.4
  16.4 0.0 copy-start.5
  16.5 0.0 copy-start.9
  16.5 0.0 copy-start.10
  16.5 5.7 %halo.1 = (bf16[176,512]{1,0:T(8,128)(2,1)S(1)}, bf16[176,512]{1,0:T(8,128)(2,1)S(1)}) custom-call(bf16[136,1024]{1,0:T(8,128)(2,1)S(1)} %collective-permute-done.halo, bf16[320,1024]{1,0:T(8,128)(2,1)S(1)} %copy-done.3, f32[1,1024]{1,0:T(1,128)S(1)} %bitcast.6, f32[1,1024]{1,0:T(1,128)S(1)} %bitcast.9, bf16[3,1024,512]{2,1,0:T(8,128)(2,1)S(1)} %copy-done.1, ...), custom_call_target="tpu_custom_call" | custom-call | flops 1500000000 | bytes 10000000 | tf_op jit(solution)/shard_map/halo/pallas_call | solution.py:241
  22.2 0.1 collective-permute-start.3
  22.3 1.4 %collective-permute-done.3.got = bf16[176,512]{1,0:T(8,128)(2,1)S(1)} collective-permute-done((bf16[176,512]{1,0:T(8,128)(2,1)S(1)}, bf16[176,512]{1,0:T(8,128)(2,1)S(1)}, u32[]{:S(2)}, u32[]{:S(2)}) %collective-permute-start.3) | collective-permute-done | bytes 180256 | tf_op jit(solution)/shard_map/ppermute | solution.py:258
  23.7 0.0 copy-done.5
  23.7 0.0 copy-done.9
  23.7 0.0 copy-done.10
  23.7 2.0 %conv.1 = bf16[320,512]{1,0:T(8,128)(2,1)} custom-call(bf16[176,512]{1,0:T(8,128)(2,1)S(1)} %get-tuple-element.31.keep, bf16[176,512]{1,0:T(8,128)(2,1)S(1)} %collective-permute-done.3.got, s32[1,320]{1,0:T(1,128)S(1)} %reshape.17.valid, f32[9,512]{1,0:T(8,128)S(1)} %copy-done.5, f32[1,512]{1,0:T(1,128)S(1)} %bitcast.10, f32[1,512]{1,0:T(1,128)S(1)} %bitcast.11), custom_call_target="tpu_custom_call" | custom-call | tf_op jit(solution)/shard_map/conv/pallas_call | solution.py:259
Async XLA Ops:
  0.0 13.9 %collective-permute-start.1 = (bf16[3,1024,512]{2,1,0:T(8,128)(2,1)}, bf16[3,1024,512]{2,1,0:T(8,128)(2,1)S(1)}, u32[]{:S(2)}, u32[]{:S(2)}) collective-permute-start(bf16[3,1024,512]{2,1,0:T(8,128)(2,1)} %refs_0_.1), channel_id=1, source_target_pairs={{0,1},{1,0},{2,3},{3,2},{4,5},{5,4},{6,7},{7,6},{8,9},{9,8},{10,11... | collective-permute-start | bytes 9437192 | tf_op jit(solution)/shard_map/ppermute | solution.py:212
  0.5 15.9 %collective-permute-start.2 = (bf16[1024,512]{1,0:T(8,128)(2,1)}, bf16[1024,512]{1,0:T(8,128)(2,1)}, u32[]{:S(2)}, u32[]{:S(2)}) collective-permute-start(bf16[1024,512]{1,0:T(8,128)(2,1)} %refs_1_.1), channel_id=1, source_target_pairs={{0,1},{1,0},{2,3},{3,2},{4,5},{5,4},{6,7},{7,6},{8,9},{9,8},{10,11... | collective-permute-start | bytes 3145736 | tf_op jit(solution)/shard_map/ppermute | solution.py:213
  1.5 14.9 %collective-permute-start = (bf16[136,1024]{1,0:T(8,128)(2,1)S(1)}, bf16[136,1024]{1,0:T(8,128)(2,1)S(1)}, u32[]{:S(2)}, u32[]{:S(2)}) collective-permute-start(bf16[136,1024]{1,0:T(8,128)(2,1)S(1)} %constant_dynamic-slice_fusion), channel_id=1, source_target_pairs={{0,2},{3,1},{2,4},{5,3},{4,6},{7,5},{6,8},{9,7},{8,10},{11,9},{10,... | collective-permute-start | bytes 835592 | tf_op jit(solution)/shard_map/ppermute | solution.py:211
  7.1 1.9 %copy-start = (bf16[3,1024,512]{2,1,0:T(8,128)(2,1)S(1)}, bf16[3,1024,512]{2,1,0:T(8,128)(2,1)}, u32[]{:S(2)}) copy-start(bf16[3,1024,512]{2,1,0:T(8,128)(2,1)} %refs_0_.1) | copy-start | bytes 9437188
  9.0 1.1 %copy-start.2 = (bf16[320,1024]{1,0:T(8,128)(2,1)S(1)}, bf16[320,1024]{1,0:T(8,128)(2,1)}, u32[]{:S(2)}) copy-start(bf16[320,1024]{1,0:T(8,128)(2,1)} %frames.5) | copy-start | bytes 1966084
  10.0 0.7 %copy-start.6 = (f32[1024]{0:T(1024)S(1)}, f32[1024]{0:T(1024)}, u32[]{:S(2)}) copy-start(f32[1024]{0:T(1024)} %param.11) | copy-start | bytes 12292
  10.7 0.7 %copy-start.7 = (f32[1024]{0:T(1024)S(1)}, f32[1024]{0:T(1024)}, u32[]{:S(2)}) copy-start(f32[1024]{0:T(1024)} %param.12) | copy-start | bytes 12292
  11.4 2.5 %copy-start.8 = (f32[1024]{0:T(1024)S(1)}, f32[1024]{0:T(1024)}, u32[]{:S(2)}) copy-start(f32[1024]{0:T(1024)} %param.12) | copy-start | bytes 12292
  13.9 2.5 %copy-start.1 = (bf16[3,1024,512]{2,1,0:T(8,128)(2,1)S(1)}, bf16[3,1024,512]{2,1,0:T(8,128)(2,1)}, u32[]{:S(2)}) copy-start(bf16[3,1024,512]{2,1,0:T(8,128)(2,1)} %refs_0_.1) | copy-start | bytes 9437188
  13.9 2.5 %copy-start.3 = (bf16[320,1024]{1,0:T(8,128)(2,1)S(1)}, bf16[320,1024]{1,0:T(8,128)(2,1)}, u32[]{:S(2)}) copy-start(bf16[320,1024]{1,0:T(8,128)(2,1)} %frames.5) | copy-start | bytes 1966084
  13.9 2.5 %copy-start.4 = (bf16[1024,512]{1,0:T(8,128)(2,1)S(1)}, bf16[1024,512]{1,0:T(8,128)(2,1)}, u32[]{:S(2)}) copy-start(bf16[1024,512]{1,0:T(8,128)(2,1)} %refs_1_.1) | copy-start | bytes 3145732
  16.4 7.2 %copy-start.5 = (f32[9,512]{1,0:T(8,128)S(1)}, f32[9,512]{1,0:T(8,128)}, u32[]{:S(2)}) copy-start(f32[9,512]{1,0:T(8,128)} %weight.1) | copy-start | bytes 55300
  16.5 7.2 %copy-start.9 = (f32[512]{0:T(512)S(1)}, f32[512]{0:T(512)}, u32[]{:S(2)}) copy-start(f32[512]{0:T(512)} %param.16) | copy-start | bytes 6148
  16.5 7.2 %copy-start.10 = (f32[512]{0:T(512)S(1)}, f32[512]{0:T(512)}, u32[]{:S(2)}) copy-start(f32[512]{0:T(512)} %param.17) | copy-start | bytes 6148
  22.2 1.5 %collective-permute-start.3 = (bf16[176,512]{1,0:T(8,128)(2,1)S(1)}, bf16[176,512]{1,0:T(8,128)(2,1)S(1)}, u32[]{:S(2)}, u32[]{:S(2)}) collective-permute-start(bf16[176,512]{1,0:T(8,128)(2,1)S(1)} %get-tuple-element.32), channel_id=1, source_target_pairs={{0,1},{1,0},{2,3},{3,2},{4,5},{5,4},{6,7},{7,6},{8,9},{9,8},{10,11... | collective-permute-start | bytes 540680 | tf_op jit(solution)/shard_map/ppermute | solution.py:258

commit v2 on v0

v2 whole, which is shorter than its diff:
```python
import math

import jax
import jax.numpy as jnp
from jax import lax
from jax.experimental import pallas as pl
from jax.experimental.pallas import tpu as pltpu
from jax.sharding import PartitionSpec as P

HEAD_DIM = 128
CTX = 128
KERNEL = 9
EXT = 8
HALO = CTX + EXT
PAD = 16
SPAN = CTX + PAD + CTX
NEG = -1e30
SCALE = math.log2(math.e) / math.sqrt(HEAD_DIM)
VMEM = pl.BlockSpec(memory_space=pltpu.VMEM)
ANY = pl.BlockSpec(memory_space=pl.ANY)
SMEM = pl.BlockSpec(memory_space=pltpu.SMEM)
F32, BF16 = jnp.float32, jnp.bfloat16


def layer_normed(values, gain, bias):
    center = values - jnp.mean(values, axis=-1, keepdims=True)
    spread = jnp.mean(center * center, axis=-1, keepdims=True)
    return center * lax.rsqrt(spread + 1e-05) * gain + bias


def dot(a, b):
    return jnp.dot(a, b, preferred_element_type=F32)


def dot_t(a, b):
    return lax.dot_general(a, b, (((1,), (1,)), ((), ())), preferred_element_type=F32)


def positions(shape, dim, start):
    return lax.broadcasted_iota(jnp.int32, shape, dim) + start


def rows_at(start, size):
    return pl.ds(pl.multiple_of(start, 8), size)


def pick_kernel(frames, sent):
    p = lax.axis_index("mp")
    sent[...] = frames[rows_at((1 - p) * (frames.shape[0] - HALO), HALO), :]


def own_heads(normed, w, count, q_out, k_out, v_out, top_out, total_out, acc_out, att_out):
    p = lax.axis_index("mp")
    keys, queries = k_out.shape[0], q_out.shape[0]
    rows = 2 * (queries - EXT)
    key_at, query_at = p * (rows - keys), p * (rows - queries)
    k_out[...] = dot(normed[...], w[1]).astype(BF16)
    picked = normed[pl.ds(pl.multiple_of(p * (keys - queries), 16), queries), :]
    q_out[...] = dot(picked, w[0]).astype(BF16)
    v_out[...] = dot(normed[...], w[2]).astype(BF16)
    key_pos = positions((queries, keys), 1, key_at)
    query_pos = positions((queries, keys), 0, query_at)
    allowed = (jnp.abs(key_pos - query_pos) <= CTX) & (key_pos < count)
    for head in range(q_out.shape[1] // HEAD_DIM):
        at = slice(head * HEAD_DIM, (head + 1) * HEAD_DIM)
        scores = dot_t(q_out[:, at], k_out[:, at]) * SCALE
        scores = jnp.where(allowed, scores, NEG)
        top = jnp.max(scores, axis=-1, keepdims=True)
        raised = jnp.exp2(scores - top)
        total = jnp.sum(raised, axis=-1, keepdims=True)
        top_out[head] = jnp.broadcast_to(top, (queries, HEAD_DIM))
        total_out[head] = jnp.broadcast_to(total, (queries, HEAD_DIM))
        acc = dot(raised.astype(BF16), v_out[:, at])
        acc_out[:, at] = acc
        att_out[:, at] = (acc * (1.0 / total)).astype(BF16)


def first_kernel(
    frames, valid, gain, bias, w, q, k, v, top, total, acc, att, normed, count_here
):
    p = lax.axis_index("mp")
    rows, keys = frames.shape[0], normed.shape[0]
    low, high = jnp.int32(0), jnp.int32(rows)
    for _ in range(rows.bit_length()):
        middle = (low + high) // 2
        one = valid[jnp.minimum(middle, rows - 1)] > 0
        open_ = low < high
        low = jnp.where(open_ & one, middle + 1, low)
        high = jnp.where(open_ & jnp.logical_not(one), middle, high)
    count = low
    count_here[...] = jnp.full(count_here.shape, count, jnp.int32)
    values = frames[rows_at(p * (rows - keys), keys), :].astype(F32)
    normed[...] = layer_normed(values, gain[...], bias[...]).astype(BF16)
    own_heads(normed, w, count, q, k, v, top, total, acc, att)


def shift_matrix(out, core, count):
    half = out.shape[0] // KERNEL
    width = out.shape[1]
    queries = width - EXT
    rows = 2 * half
    tm, last = lax.axis_index("tm"), lax.axis_size("tm") - 1
    column = positions((1, width), 1, 0)
    edge = jnp.where(core == 0, -EXT, rows)
    time = jnp.where(column < queries, column + core * (rows - queries), column - queries + edge)
    low = jnp.where(tm > 0, -EXT, 0)
    high = jnp.where(tm < last, rows + EXT, count[0:1, :width])
    time = jnp.where((time >= low) & (time < high), time, -rows)
    for tap in range(KERNEL):
        row = positions((half, width), 0, core * half + tap - KERNEL // 2)
        out[tap * half : (tap + 1) * half, :] = jnp.where(row == time, 1.0, 0.0).astype(BF16)


def second_kernel(
    normed, w, count_here, q, k, v, top, total, acc, att, own_shift, other_shift
):
    p = lax.axis_index("mp")
    keys = k.shape[0]
    count = jnp.concatenate([count_here[0:1, :]] * pl.cdiv(keys, count_here.shape[1]), axis=1)[:, :keys]
    own_heads(normed, w, count, q, k, v, top, total, acc, att)
    shift_matrix(own_shift, p, count_here)
    shift_matrix(other_shift, 1 - p, count_here)


def halo_kernel(halo, frames, gain, bias, wo_a, wo_b, *refs):
    parts = (refs[:8], refs[8:16])
    keep, send, normed, far_normed, kx, vx, att_all = refs[16:]
    p = lax.axis_index("mp")
    last = lax.axis_size("tm") - 1
    tm = lax.axis_index("tm")
    rows, queries, keys = frames.shape[0], refs[1].shape[0], refs[2].shape[0]
    width = refs[1].shape[1]
    heads = width // HEAD_DIM
    present = jnp.where(p == 0, tm > 0, tm < last)
    near = halo[rows_at(EXT * (1 - p), CTX), :].astype(F32)
    far = halo[rows_at(CTX * p, EXT), :].astype(F32)
    values = layer_normed(jnp.concatenate([near, far], axis=0), gain[...], bias[...])
    far_normed[...] = values
    normed[...] = values.astype(BF16)
    ext_normed = far_normed[rows_at((CTX - EXT) * (1 - p), EXT), :].astype(BF16)
    near_at = jnp.where(p == 0, -CTX, rows)
    far_at = jnp.where(p == 0, -HALO, rows + CTX)
    ext_at = jnp.where(p == 0, -EXT, rows)
    part = rows_at(p * (queries - CTX), CTX)
    own = rows_at(p * (keys - CTX), CTX)
    own_pos = p * (rows - CTX)
    blank = jnp.zeros((PAD - EXT, width), F32)
    q_ext = []
    for side, (w, q, k, v, top_own, total_own, acc_own, att) in enumerate(parts):
        to = slice(side * width, (side + 1) * width)
        kx[CTX + PAD :, to] = k[own, :]
        vx[CTX + PAD :, to] = v[own, :]
        att_all[:queries, to] = att[...]
    for side, (w, q, k, v, top_own, total_own, acc_own, att) in enumerate(parts):
        to = slice(side * width, (side + 1) * width)
        for x, i in ((kx, 1), (vx, 2)):
            got = dot(normed[...], w[i])
            x[:CTX, to] = got[:CTX].astype(BF16)
            x[CTX : CTX + PAD, to] = jnp.concatenate([got[CTX:], blank], axis=0).astype(BF16)
        q_ext.append(dot(ext_normed, w[0]))
    q_ext = jnp.concatenate(q_ext, axis=1)
    deep = 2 * heads * EXT
    tiled = jnp.concatenate([q_ext] * (2 * heads), axis=0)
    head_of_row = positions(tiled.shape, 0, 0) // EXT
    head_of_lane = positions(tiled.shape, 1, 0) // HEAD_DIM
    tiled = jnp.where(head_of_row == head_of_lane, tiled, 0.0).astype(BF16)
    column = positions((deep, SPAN), 1, 0)
    key_pos = jnp.where(
        column < CTX,
        column + near_at,
        jnp.where(column < CTX + EXT, column - CTX + far_at, column - (CTX + PAD) + own_pos),
    )
    row_pos = positions((deep, SPAN), 0, 0) % EXT + ext_at
    seen = (jnp.abs(key_pos - row_pos) <= CTX) & ((column < CTX + EXT) | (column >= CTX + PAD))
    scores = jnp.where(seen, dot_t(tiled, kx[...]) * SCALE, NEG)
    top = jnp.max(scores, axis=-1, keepdims=True)
    raised = jnp.exp2(scores - top)
    total = jnp.sum(raised, axis=-1, keepdims=True)
    spread = dot(raised.astype(BF16), vx[...]) * (1.0 / total)
    ext_att = jnp.concatenate(
        [
            spread[h * EXT : (h + 1) * EXT, h * HEAD_DIM : (h + 1) * HEAD_DIM]
            for h in range(2 * heads)
        ],
        axis=1,
    )
    query_pos = positions((CTX, CTX), 0, p * (rows - CTX))
    near_pos = positions((CTX, CTX), 1, near_at)
    allowed = (jnp.abs(near_pos - query_pos) <= CTX) & present
    for side, (w, q, k, v, top_own, total_own, acc_own, att) in enumerate(parts):
        for head in range(heads):
            at = slice(head * HEAD_DIM, (head + 1) * HEAD_DIM)
            to = slice(side * width + at.start, side * width + at.stop)
            scores = dot_t(q[part, at], kx[:CTX, to]) * SCALE
            scores = jnp.where(allowed, scores, NEG)
            before = top_own[head, part, :]
            top = jnp.maximum(before, jnp.max(scores, axis=-1, keepdims=True))
            raised = jnp.exp2(scores - top)
            faded = jnp.exp2(before - top)
            total = total_own[head, part, :] * faded + jnp.sum(raised, axis=-1, keepdims=True)
            acc = acc_own[part, at] * faded + dot(raised.astype(BF16), vx[:CTX, to])
            att_all[part, to] = (acc / total).astype(BF16)
    ext_att = jnp.concatenate([ext_att, jnp.zeros_like(ext_att)], axis=0).astype(BF16)
    here = pl.ds(pl.multiple_of(p * width, width), width)
    there = pl.ds(pl.multiple_of((1 - p) * width, width), width)
    own_rows = rows_at(p * (rows - queries), queries)
    ext_rows = rows_at(CTX * (1 - p), EXT)
    for wo, columns, out in ((wo_b, there, send), (wo_a, here, keep)):
        projected = dot(att_all[:, :width], wo[here, :]) + dot(att_all[:, width:], wo[there, :])
        out[:queries] = (frames[own_rows, columns].astype(F32) + projected).astype(BF16)
        edge = dot(ext_att[:, :width], wo[here, :]) + dot(ext_att[:, width:], wo[there, :])
        out[queries:] = (halo[ext_rows, columns].astype(F32) + edge[:EXT]).astype(BF16)


def convolved(block, core, shift_by, weight, scale, shift, store):
    half = shift_by.shape[0] // KERNEL
    queries = block.shape[0] - EXT
    rows = rows_at(core * (queries - half), half)
    step = 256
    for at in range(0, block.shape[1], step):
        lanes = slice(at, at + step)
        gain = 0.5 * scale[:, lanes]
        u = jnp.broadcast_to(0.5 * shift[:, lanes], (half, step))
        for tap in range(KERNEL):
            moved = dot(shift_by[tap * half : (tap + 1) * half, :], block[:, lanes])
            u = u + moved * (weight[tap : tap + 1, lanes] * gain)
        plain = block[rows, lanes].astype(F32)
        store(lanes, (plain + (u + u * jnp.tanh(u))).astype(BF16))


def own_conv_kernel(keep, shift_by, weight, scale, shift, out):
    def store(lanes, value):
        out[:, lanes] = value

    convolved(keep, lax.axis_index("mp"), shift_by, weight, scale, shift, store)


def other_conv_kernel(got, done, shift_by, weight, scale, shift, out, block, sems):
    core = 1 - lax.axis_index("mp")
    half = done.shape[0]
    first = pltpu.make_async_copy(done, out.at[rows_at((1 - core) * half, half), :], sems.at[0])
    first.start()
    copies = [first]

    def store(lanes, value):
        block[:, lanes] = value
        copies.append(
            pltpu.make_async_copy(
                block.at[:, lanes], out.at[rows_at(core * half, half), lanes], sems.at[len(copies)]
            )
        )
        copies[-1].start()

    convolved(got, core, shift_by, weight, scale, shift, store)
    for copy in copies:
        copy.wait()


def call(kernel, name, out_shape, in_specs, out_specs, scratch=(), flops=0, size=0, exps=0, limit=16):
    return pl.pallas_call(
        kernel,
        out_shape=out_shape,
        in_specs=in_specs,
        out_specs=out_specs,
        scratch_shapes=scratch,
        compiler_params=pltpu.CompilerParams(vmem_limit_bytes=limit << 20),
        cost_estimate=pl.CostEstimate(flops=flops, bytes_accessed=size, transcendentals=exps),
        name=name,
    )


def local(frames, valid, norm_gain, norm_bias, w_qkv, w_out, conv_weight, conv_scale, conv_shift):
    rows, model = frames.shape
    width = w_qkv.shape[2]
    heads = width // HEAD_DIM
    count = lax.axis_size("tm")
    half = rows // 2
    queries = half + EXT
    keys = half + EXT + CTX
    block = queries + EXT
    assert rows >= HALO + CTX and rows % 32 == 0
    shaped = jax.ShapeDtypeStruct
    pairs = []
    for i in range(count - 1):
        pairs += [(2 * i, 2 * (i + 1)), (2 * (i + 1) + 1, 2 * i + 1)]
    other = [(0, 1), (1, 0)]
    sent = call(
        pick_kernel, "pick", shaped((HALO, model), BF16), [VMEM], VMEM, flops=5_000_000_000
    )(frames)
    halo = lax.ppermute(sent, ("tm", "mp"), pairs)
    w_other = lax.ppermute(w_qkv, "mp", other)
    wo_other = lax.ppermute(w_out, "mp", other)
    gain, bias = norm_gain.reshape(1, model), norm_bias.reshape(1, model)
    results = (
        shaped((queries, width), BF16),
        shaped((keys, width), BF16),
        shaped((keys, width), BF16),
        shaped((heads, queries, HEAD_DIM), F32),
        shaped((heads, queries, HEAD_DIM), F32),
        shaped((queries, width), F32),
        shaped((queries, width), BF16),
    )
    first = call(
        first_kernel,
        "first",
        results + (shaped((keys, model), BF16), shaped((8, 256), jnp.int32)),
        [VMEM, SMEM, VMEM, VMEM, VMEM],
        (VMEM,) * 9,
        flops=1_300_000_000,
        size=4_000_000,
        exps=300_000,
    )(frames, valid, gain, bias, w_qkv)
    mine, (normed, count_here) = first[:7], first[7:]
    second = call(
        second_kernel,
        "second",
        results + (shaped((KERNEL * half, block), BF16),) * 2,
        [VMEM] * 3,
        (VMEM,) * 9,
        flops=1_300_000_000,
        size=4_000_000,
        exps=300_000,
    )(normed, w_other, count_here)
    theirs, (own_shift, other_shift) = second[:7], second[7:]
    keep, send = call(
        halo_kernel,
        "halo",
        (shaped((block, width), BF16),) * 2,
        [VMEM] * 22,
        (VMEM,) * 2,
        [
            pltpu.VMEM((HALO, model), BF16),
            pltpu.VMEM((HALO, model), F32),
            pltpu.VMEM((SPAN, model), BF16),
            pltpu.VMEM((SPAN, model), BF16),
            pltpu.VMEM((queries, model), BF16),
        ],
        flops=1_500_000_000,
        size=10_000_000,
        exps=300_000,
    )(halo, frames, gain, bias, w_out, wo_other, w_qkv, *mine, w_other, *theirs)
    got = lax.ppermute(send, "mp", other)
    weights = (conv_weight, conv_scale.reshape(1, width), conv_shift.reshape(1, width))
    done = call(
        own_conv_kernel,
        "own_conv",
        shaped((half, width), BF16),
        [VMEM] * 5,
        VMEM,
        flops=270_000_000,
        size=1_000_000,
    )(keep, own_shift, *weights)
    return call(
        other_conv_kernel,
        "other_conv",
        shaped((rows, width), BF16),
        [VMEM] * 6,
        ANY,
        [pltpu.VMEM((half, width), BF16), pltpu.SemaphoreType.DMA((1 + width // 256,))],
        flops=270_000_000,
        size=1_000_000,
    )(got, done, other_shift, *weights)


def solution(mesh):
    placed = (
        P("tm", None),
        P("tm"),
        P(),
        P(),
        P(None, None, "mp"),
        P(None, "mp"),
        P(None, "mp"),
        P("mp"),
        P("mp"),
    )
    return jax.shard_map(
        local, mesh=mesh, in_specs=placed, out_specs=P("tm", "mp"), check_vma=False
    )
```

time: 42.6 us -> 21.5 us (0.50)
  the two profiles are of different devices: /device:TPU:22 before, /device:TPU:0 now
where the time goes in v2:
time: 21.5 us; the launch traced here: 21.3 us
  Pallas kernels  11.9 us (55%)
  starting transfers between devices  5.55 us (26%)
  waiting for transfers between devices  2.31 us (11%)
  local copies, waits for them, and re-layouts  1.41 us (7%)
    ppermute x1, starting transfers between devices, local(): halo = lax.ppermute(sent, ('tm', 'mp'), pairs)  4.95 us
    pallas_call x1, Pallas kernels, local(): call(halo_kernel, 'halo', (shaped((block, width), BF16),) * 2, [VMEM] * 2...  4.66 us
    pallas_call x1, Pallas kernels, local(): call(first_kernel, 'first', results + (shaped((keys, model), BF16), shape...  3.02 us
    pallas_call x1, Pallas kernels, local(): call(second_kernel, 'second', results + (shaped((KERNEL * half, block), B...  2.42 us
    ppermute x1, waiting for transfers between devices, local(): halo = lax.ppermute(sent, ('tm', 'mp'), pairs)  1.49 us
    unnamed x20, local copies, waits for them, and re-layouts  1.41 us
    pallas_call x1, Pallas kernels, local(): call(other_conv_kernel, 'other_conv', shaped((rows, width), BF16), [VMEM]...  1.22 us
    ppermute x1, waiting for transfers between devices, local(): got = lax.ppermute(send, 'mp', other)  0.81 us
  transfers between devices with their start and end apart: 4, of which 2 were waited for; matrix products, arithmetic and copies ran while one was open for 0% of the time, Pallas kernels for 28%

profile of v2, /device:TPU:0, one launch (start us, length us, event | category | flops | bytes accessed | tf_op | source)
XLA Modules:
  0.0 21.3 jit_solution(15150638365918254154)
XLA Ops:
  0.0 0.0 copy-start
  0.0 0.5 %collective-permute-start.2 = (bf16[3,1024,512]{2,1,0:T(8,128)(2,1)}, bf16[3,1024,512]{2,1,0:T(8,128)(2,1)S(1)}, u32[]{:S(2)}, u32[]{:S(2)}) collective-permute-start(bf16[3,1024,512]{2,1,0:T(8,128)(2,1)} %refs_0_.1), channel_id=1, source_target_pairs={{0,1},{1,0},{2,3},{3,2},{4,5},{5,4},{6,7},{7,6},{8,9},{9,8},{10,11... | collective-permute-start | bytes 9437192 | tf_op jit(solution)/shard_map/ppermute | solution.py:291
  0.5 0.1 collective-permute-start.1
  0.6 0.0 copy-start.2
  0.6 1.4 %copy-done.2 = bf16[320,1024]{1,0:T(8,128)(2,1)S(1)} copy-done((bf16[320,1024]{1,0:T(8,128)(2,1)S(1)}, bf16[320,1024]{1,0:T(8,128)(2,1)}, u32[]{:S(2)}) %copy-start.2) | copy-done | bytes 655384
  1.9 0.0 copy-start.7
  1.9 0.0 copy-start.8
  1.9 0.0 copy-start.9
  2.0 5.0 %collective-permute-start = (bf16[136,1024]{1,0:T(8,128)(2,1)S(1)}, bf16[136,1024]{1,0:T(8,128)(2,1)S(1)}, u32[]{:S(2)}, u32[]{:S(2)}) collective-permute-start(bf16[136,1024]{1,0:T(8,128)(2,1)S(1)} %pick.1), channel_id=1, source_target_pairs={{0,2},{3,1},{2,4},{5,3},{4,6},{7,5},{6,8},{9,7},{8,10},{11,9},{10,... | collective-permute-start | bytes 835592 | tf_op jit(solution)/shard_map/ppermute | solution.py:290
  6.9 0.0 copy-done
  6.9 0.0 copy-done.7
  6.9 0.0 copy-done.8
  6.9 0.0 copy-done.9
  7.0 3.0 %first.1 = (bf16[168,512]{1,0:T(8,128)(2,1)S(1)}, bf16[296,512]{1,0:T(8,128)(2,1)S(1)}, bf16[296,512]{1,0:T(8,128)(2,1)S(1)}, f32[4,168,128]{2,1,0:T(8,128)S(1)}...) custom-call(bf16[320,1024]{1,0:T(8,128)(2,1)S(1)} %copy-done.2, ...), custom_call_target="tpu_custom_call" | custom-call | flops 1300000000 | bytes 4000000 | tf_op jit(solution)/shard_map/first/pallas_call | solution.py:303
  10.0 0.0 copy-start.1
  10.0 0.0 copy-start.3
  10.0 0.0 collective-permute-done.2.w.refs_8_
  10.0 2.4 %second.1 = (bf16[168,512]{1,0:T(8,128)(2,1)S(1)}, bf16[296,512]{1,0:T(8,128)(2,1)S(1)}, bf16[296,512]{1,0:T(8,128)(2,1)S(1)}, f32[4,168,128]{2,1,0:T(8,128)S(1)...) custom-call(bf16[296,1024]{1,0:T(8,128)(2,1)S(1)} %get-tuple-element, ...), custom_call_target="tpu_custom_call" | custom-call | flops 1300000000 | bytes 4000000 | tf_op jit(solution)/shard_map/second/pallas_call | solution.py:314
  12.4 1.5 %collective-permute-done.halo = bf16[136,1024]{1,0:T(8,128)(2,1)S(1)} collective-permute-done((bf16[136,1024]{1,0:T(8,128)(2,1)S(1)}, bf16[136,1024]{1,0:T(8,128)(2,1)S(1)}, u32[]{:S(2)}, u32[]{:S(2)}) %collective-permute-start) | collective-permute-done | bytes 278560 | tf_op jit(solution)/shard_map/ppermute | solution.py:290
  13.9 0.0 collective-permute-done.1.wo_b
  13.9 0.0 copy-done.1
  13.9 0.0 copy-done.3
  13.9 0.0 copy-start.4
  13.9 0.0 copy-start.5
  14.0 0.0 copy-start.6
  14.0 4.7 %halo.1 = (bf16[176,512]{1,0:T(8,128)(2,1)S(1)}, bf16[176,512]{1,0:T(8,128)(2,1)S(1)}) custom-call(bf16[136,1024]{1,0:T(8,128)(2,1)S(1)} %collective-permute-done.halo, bf16[320,1024]{1,0:T(8,128)(2,1)S(1)} %copy-done.3, f32[1,1024]{1,0:T(1,128)S(1)} %bitcast.9, f32[1,1024]{1,0:T(1,128)S(1)} %bitcast.11, bf16[1024,512]{1,0:T(8,128)(2,1)S(1)} %copy-done.1, ...), custom_call_target="tpu_custom_call" | custom-call | flops 1500000000 | bytes 10000000 | tf_op jit(solution)/shard_map/halo/pallas_call | solution.py:325
  18.6 0.0 collective-permute-start.3
  18.7 0.0 copy-done.4
  18.7 0.0 copy-done.5
  18.7 0.0 copy-done.6
  18.7 0.6 %own_conv.1.done = bf16[160,512]{1,0:T(8,128)(2,1)S(1)} custom-call(bf16[176,512]{1,0:T(8,128)(2,1)S(1)} %get-tuple-element.42.keep, bf16[1440,176]{1,0:T(8,128)(2,1)S(1)} %get-tuple-element.43.shift_by, f32[9,512]{1,0:T(8,128)S(1)} %copy-done.4, f32[1,512]{1,0:T(1,128)S(1)} %bitcast.4, f32[1,512]{1,0:T(1,128)S(1)} %bitcast.6), custom_call_target="tpu_custom_call" | custom-call | flops 270000000 | bytes 1000000 | tf_op jit(solution)/shard_map/own_conv/pallas_call | solution.py:344
  19.3 0.8 %collective-permute-done.3.got = bf16[176,512]{1,0:T(8,128)(2,1)S(1)} collective-permute-done((bf16[176,512]{1,0:T(8,128)(2,1)S(1)}, bf16[176,512]{1,0:T(8,128)(2,1)S(1)}, u32[]{:S(2)}, u32[]{:S(2)}) %collective-permute-start.3) | collective-permute-done | bytes 180256 | tf_op jit(solution)/shard_map/ppermute | solution.py:342
  20.1 1.2 %other_conv.1 = bf16[320,512]{1,0:T(8,128)(2,1)} custom-call(bf16[176,512]{1,0:T(8,128)(2,1)S(1)} %collective-permute-done.3.got, bf16[160,512]{1,0:T(8,128)(2,1)S(1)} %own_conv.1.done, bf16[1440,176]{1,0:T(8,128)(2,1)S(1)} %get-tuple-element.44.shift_by, f32[9,512]{1,0:T(8,128)S(1)} %copy-done.4, f32[1,512]{1,0:T(1,128)S(1)} %bitcast.5, f32[1,512]{1,0:T(1,128)S(1)} %bitcast.7), custom_call_target="tpu_custom_call" | custom-call | flops 270000000 | bytes 1000000 | tf_op jit(solution)/shard_map/other_conv/pallas_call | solution.py:353
  (1 shorter events, 0.0 us)
Async XLA Ops:
  0.0 6.9 %copy-start = (bf16[3,1024,512]{2,1,0:T(8,128)(2,1)S(1)}, bf16[3,1024,512]{2,1,0:T(8,128)(2,1)}, u32[]{:S(2)}) copy-start(bf16[3,1024,512]{2,1,0:T(8,128)(2,1)} %refs_0_.1) | copy-start | bytes 9437188
  0.0 10.0 %collective-permute-start.2 = (bf16[3,1024,512]{2,1,0:T(8,128)(2,1)}, bf16[3,1024,512]{2,1,0:T(8,128)(2,1)S(1)}, u32[]{:S(2)}, u32[]{:S(2)}) collective-permute-start(bf16[3,1024,512]{2,1,0:T(8,128)(2,1)} %refs_0_.1), channel_id=1, source_target_pairs={{0,1},{1,0},{2,3},{3,2},{4,5},{5,4},{6,7},{7,6},{8,9},{9,8},{10,11... | collective-permute-start | bytes 9437192 | tf_op jit(solution)/shard_map/ppermute | solution.py:291
  0.5 13.4 %collective-permute-start.1 = (bf16[1024,512]{1,0:T(8,128)(2,1)}, bf16[1024,512]{1,0:T(8,128)(2,1)S(1)}, u32[]{:S(2)}, u32[]{:S(2)}) collective-permute-start(bf16[1024,512]{1,0:T(8,128)(2,1)} %wo_a.1), channel_id=1, source_target_pairs={{0,1},{1,0},{2,3},{3,2},{4,5},{5,4},{6,7},{7,6},{8,9},{9,8},{10,11... | collective-permute-start | bytes 3145736 | tf_op jit(solution)/shard_map/ppermute | solution.py:292
  0.6 1.4 %copy-start.2 = (bf16[320,1024]{1,0:T(8,128)(2,1)S(1)}, bf16[320,1024]{1,0:T(8,128)(2,1)}, u32[]{:S(2)}) copy-start(bf16[320,1024]{1,0:T(8,128)(2,1)} %frames.5) | copy-start | bytes 1966084
  1.9 5.0 %copy-start.7 = (f32[1024]{0:T(1024)S(1)}, f32[1024]{0:T(1024)}, u32[]{:S(2)}) copy-start(f32[1024]{0:T(1024)} %param.11) | copy-start | bytes 12292
  1.9 5.0 %copy-start.8 = (f32[1024]{0:T(1024)S(1)}, f32[1024]{0:T(1024)}, u32[]{:S(2)}) copy-start(f32[1024]{0:T(1024)} %param.12) | copy-start | bytes 12292
  1.9 5.0 %copy-start.9 = (s32[320]{0:T(512)S(1)}, s32[320]{0:T(512)}, u32[]{:S(2)}) copy-start(s32[320]{0:T(512)} %valid.1) | copy-start | bytes 3844
  2.0 12.0 %collective-permute-start = (bf16[136,1024]{1,0:T(8,128)(2,1)S(1)}, bf16[136,1024]{1,0:T(8,128)(2,1)S(1)}, u32[]{:S(2)}, u32[]{:S(2)}) collective-permute-start(bf16[136,1024]{1,0:T(8,128)(2,1)S(1)} %pick.1), channel_id=1, source_target_pairs={{0,2},{3,1},{2,4},{5,3},{4,6},{7,5},{6,8},{9,7},{8,10},{11,9},{10,... | collective-permute-start | bytes 835592 | tf_op jit(solution)/shard_map/ppermute | solution.py:290
  10.0 4.0 %copy-start.1 = (bf16[1024,512]{1,0:T(8,128)(2,1)S(1)}, bf16[1024,512]{1,0:T(8,128)(2,1)}, u32[]{:S(2)}) copy-start(bf16[1024,512]{1,0:T(8,128)(2,1)} %wo_a.1) | copy-start | bytes 3145732
  10.0 3.9 %copy-start.3 = (bf16[320,1024]{1,0:T(8,128)(2,1)S(1)}, bf16[320,1024]{1,0:T(8,128)(2,1)}, u32[]{:S(2)}) copy-start(bf16[320,1024]{1,0:T(8,128)(2,1)} %frames.5) | copy-start | bytes 1966084
  13.9 4.7 %copy-start.4 = (f32[9,512]{1,0:T(8,128)S(1)}, f32[9,512]{1,0:T(8,128)}, u32[]{:S(2)}) copy-start(f32[9,512]{1,0:T(8,128)} %weight.3) | copy-start | bytes 55300
  13.9 4.8 %copy-start.5 = (f32[512]{0:T(512)S(1)}, f32[512]{0:T(512)}, u32[]{:S(2)}) copy-start(f32[512]{0:T(512)} %param.16) | copy-start | bytes 6148
  14.0 4.7 %copy-start.6 = (f32[512]{0:T(512)S(1)}, f32[512]{0:T(512)}, u32[]{:S(2)}) copy-start(f32[512]{0:T(512)} %param.17) | copy-start | bytes 6148
  18.6 1.5 %collective-permute-start.3 = (bf16[176,512]{1,0:T(8,128)(2,1)S(1)}, bf16[176,512]{1,0:T(8,128)(2,1)S(1)}, u32[]{:S(2)}, u32[]{:S(2)}) collective-permute-start(bf16[176,512]{1,0:T(8,128)(2,1)S(1)} %get-tuple-element.41), channel_id=1, source_target_pairs={{0,1},{1,0},{2,3},{3,2},{4,5},{5,4},{6,7},{7,6},{8,9},{9,8},{10,11... | collective-permute-start | bytes 540680 | tf_op jit(solution)/shard_map/ppermute | solution.py:342

commit v3 on v2

v3 whole, which is shorter than its diff:
```python
import math

import jax
import jax.numpy as jnp
from jax import lax
from jax.experimental import pallas as pl
from jax.experimental.pallas import tpu as pltpu
from jax.sharding import PartitionSpec as P

HEAD_DIM = 128
CTX = 128
KERNEL = 9
EXT = 8
HALO = CTX + EXT
PAD = 16
SPAN = CTX + PAD + CTX
NEG = -1e30
WARM_FLOPS, PICK_FLOPS, NORM_FLOPS = 1_500_000_000, 1_000_000_000, 1_500_000_000
SCALE = math.log2(math.e) / math.sqrt(HEAD_DIM)
VMEM = pl.BlockSpec(memory_space=pltpu.VMEM)
ANY = pl.BlockSpec(memory_space=pl.ANY)
SMEM = pl.BlockSpec(memory_space=pltpu.SMEM)
F32, BF16 = jnp.float32, jnp.bfloat16


def layer_normed(values, gain, bias):
    center = values - jnp.mean(values, axis=-1, keepdims=True)
    spread = jnp.mean(center * center, axis=-1, keepdims=True)
    return center * lax.rsqrt(spread + 1e-05) * gain + bias


def norm_rows(source, source_at, target, target_at, count, gain, bias):
    step = 16
    for at in range(0, count, step):
        size = min(step, count - at)
        values = source[rows_at(source_at + at, size), :].astype(F32)
        target[target_at + at : target_at + at + size, :] = layer_normed(
            values, gain, bias
        ).astype(BF16)


def dot(a, b):
    return jnp.dot(a, b, preferred_element_type=F32)


def dot_t(a, b):
    return lax.dot_general(a, b, (((1,), (1,)), ((), ())), preferred_element_type=F32)


def positions(shape, dim, start):
    return lax.broadcasted_iota(jnp.int32, shape, dim) + start


def rows_at(start, size):
    return pl.ds(pl.multiple_of(start, 8), size)


def pick_kernel(frames, after, sent):
    p = lax.axis_index("mp")
    sent[...] = frames[rows_at((1 - p) * (frames.shape[0] - HALO), HALO), :]


def own_heads(normed, w, count, q_out, k_out, v_out, top_out, total_out, acc_out, att_out):
    p = lax.axis_index("mp")
    keys, queries = k_out.shape[0], q_out.shape[0]
    rows = 2 * (queries - EXT)
    key_at, query_at = p * (rows - keys), p * (rows - queries)
    k_out[...] = dot(normed[...], w[1]).astype(BF16)
    picked = normed[pl.ds(pl.multiple_of(p * (keys - queries), 16), queries), :]
    q_out[...] = (dot(picked, w[0]) * SCALE).astype(BF16)
    v_out[...] = dot(normed[...], w[2]).astype(BF16)
    key_pos = positions((queries, keys), 1, key_at)
    query_pos = positions((queries, keys), 0, query_at)
    allowed = (jnp.abs(key_pos - query_pos) <= CTX) & (key_pos < count)
    for head in range(q_out.shape[1] // HEAD_DIM):
        at = slice(head * HEAD_DIM, (head + 1) * HEAD_DIM)
        scores = dot_t(q_out[:, at], k_out[:, at])
        scores = jnp.where(allowed, scores, NEG)
        top = jnp.max(scores, axis=-1, keepdims=True)
        raised = jnp.exp2(scores - top)
        total = jnp.sum(raised, axis=-1, keepdims=True)
        top_out[head] = jnp.broadcast_to(top, (queries, HEAD_DIM))
        total_out[head] = jnp.broadcast_to(total, (queries, HEAD_DIM))
        acc = dot(raised.astype(BF16), v_out[:, at])
        acc_out[:, at] = acc
        att_out[:, at] = (acc * (1.0 / total)).astype(BF16)


def norm_kernel(frames, valid, gain, bias, normed, count_here):
    p = lax.axis_index("mp")
    rows, keys = frames.shape[0], normed.shape[0]
    low, high = jnp.int32(0), jnp.int32(rows)
    for _ in range(rows.bit_length()):
        middle = (low + high) // 2
        one = valid[jnp.minimum(middle, rows - 1)] > 0
        open_ = low < high
        low = jnp.where(open_ & one, middle + 1, low)
        high = jnp.where(open_ & jnp.logical_not(one), middle, high)
    count_here[...] = jnp.full(count_here.shape, low, jnp.int32)
    norm_rows(frames, p * (rows - keys), normed, 0, keys, gain[...], bias[...])


def first_kernel(normed, w, count_here, q, k, v, top, total, acc, att):
    keys = k.shape[0]
    count = jnp.concatenate([count_here[0:1, :]] * pl.cdiv(keys, count_here.shape[1]), axis=1)[:, :keys]
    own_heads(normed, w, count, q, k, v, top, total, acc, att)


def warm_kernel(own_shift, other_shift):
    p = lax.axis_index("mp")
    for out, core in ((own_shift, p), (other_shift, 1 - p)):
        half, width = out.shape[0] // KERNEL, out.shape[1]
        queries, rows = width - EXT, 2 * half
        column = positions((1, width), 1, 0)
        edge = jnp.where(core == 0, -EXT, rows)
        time = jnp.where(column < queries, column + core * (rows - queries), column - queries + edge)
        for tap in range(KERNEL):
            row = positions((half, width), 0, core * half + tap - KERNEL // 2)
            out[tap * half : (tap + 1) * half, :] = jnp.where(row == time, 1.0, 0.0).astype(BF16)


def mask_shift(shift, core, count, out):
    half, width = out.shape[0] // KERNEL, out.shape[1]
    queries, rows = width - EXT, 2 * half
    tm, last = lax.axis_index("tm"), lax.axis_size("tm") - 1
    column = positions((1, width), 1, 0)
    edge = jnp.where(core == 0, -EXT, rows)
    time = jnp.where(column < queries, column + core * (rows - queries), column - queries + edge)
    low = jnp.where(tm > 0, -EXT, 0)
    high = jnp.where(tm < last, rows + EXT, count[0:1, :width])
    mask = jnp.where((time >= low) & (time < high), 1.0, 0.0).astype(BF16)
    for tap in range(KERNEL):
        at = slice(tap * half, (tap + 1) * half)
        out[at, :] = shift[at, :] * mask


def second_kernel(
    normed, w, count_here, own_base, other_base, q, k, v, top, total, acc, att, own_shift, other_shift
):
    p = lax.axis_index("mp")
    first_kernel(normed, w, count_here, q, k, v, top, total, acc, att)
    mask_shift(own_base, p, count_here, own_shift)
    mask_shift(other_base, 1 - p, count_here, other_shift)


def halo_kernel(halo, frames, gain, bias, wo, *refs):
    parts = (refs[:8], refs[8:16])
    send, att_all, normed, kx, vx = refs[16:]
    p = lax.axis_index("mp")
    last = lax.axis_size("tm") - 1
    tm = lax.axis_index("tm")
    rows, queries, keys = frames.shape[0], refs[1].shape[0], refs[2].shape[0]
    width = refs[1].shape[1]
    heads = width // HEAD_DIM
    present = jnp.where(p == 0, tm > 0, tm < last)
    norms = (gain[...], bias[...])
    ext_normed = layer_normed(halo[rows_at(CTX * (1 - p), EXT), :].astype(F32), *norms).astype(BF16)
    norm_rows(halo, EXT * (1 - p), normed, 0, CTX, *norms)
    norm_rows(halo, CTX * p, normed, CTX, EXT, *norms)
    near_at = jnp.where(p == 0, -CTX, rows)
    far_at = jnp.where(p == 0, -HALO, rows + CTX)
    ext_at = jnp.where(p == 0, -EXT, rows)
    part = rows_at(p * (queries - CTX), CTX)
    own = rows_at(p * (keys - CTX), CTX)
    own_pos = p * (rows - CTX)
    blank = jnp.zeros((PAD - EXT, width), F32)
    query_pos = positions((CTX, CTX), 0, p * (rows - CTX))
    near_pos = positions((CTX, CTX), 1, near_at)
    allowed = (jnp.abs(near_pos - query_pos) <= CTX) & present
    each = [
        (side, head, slice(head * HEAD_DIM, (head + 1) * HEAD_DIM))
        for side in range(2)
        for head in range(heads)
    ]

    def lanes_of(side, at):
        return slice(side * width + at.start, side * width + at.stop)

    for side, (w, q, k, v, top_own, total_own, acc_own, att) in enumerate(parts):
        to = slice(side * width, (side + 1) * width)
        kx[CTX + PAD :, to] = k[own, :]
        vx[CTX + PAD :, to] = v[own, :]
        att_all[:queries, to] = att[...]

    def project(x, i):
        for side, (w, *_) in enumerate(parts):
            to = slice(side * width, (side + 1) * width)
            got = dot(normed[...], w[i])
            x[:CTX, to] = got[:CTX].astype(BF16)
            x[CTX : CTX + PAD, to] = jnp.concatenate([got[CTX:], blank], axis=0).astype(BF16)

    q_ext = jnp.concatenate([dot(ext_normed, w[0]) * SCALE for w, *_ in parts], axis=1)
    project(kx, 1)
    deep = 2 * heads * EXT
    tiled = jnp.concatenate([q_ext] * (2 * heads), axis=0)
    head_of_row = positions(tiled.shape, 0, 0) // EXT
    head_of_lane = positions(tiled.shape, 1, 0) // HEAD_DIM
    tiled = jnp.where(head_of_row == head_of_lane, tiled, 0.0).astype(BF16)
    scores = [
        dot_t(parts[side][1][part, at], kx[:CTX, lanes_of(side, at)]) for side, head, at in each
    ]
    ext_scores = dot_t(tiled, kx[...])
    project(vx, 2)
    raised, total, faded = [], [], []
    for (side, head, at), score in zip(each, scores):
        top_own, total_own = parts[side][4], parts[side][5]
        score = jnp.where(allowed, score, NEG)
        before = top_own[head, part, :]
        top = jnp.maximum(before, jnp.max(score, axis=-1, keepdims=True))
        up = jnp.exp2(score - top)
        faded.append(jnp.exp2(before - top))
        total.append(
            total_own[head, part, :] * faded[-1] + jnp.sum(up, axis=-1, keepdims=True)
        )
        raised.append(up.astype(BF16))
    column = positions((deep, SPAN), 1, 0)
    key_pos = jnp.where(
        column < CTX,
        column + near_at,
        jnp.where(column < CTX + EXT, column - CTX + far_at, column - (CTX + PAD) + own_pos),
    )
    row_pos = positions((deep, SPAN), 0, 0) % EXT + ext_at
    seen = (jnp.abs(key_pos - row_pos) <= CTX) & ((column < CTX + EXT) | (column >= CTX + PAD))
    ext_scores = jnp.where(seen, ext_scores, NEG)
    ext_up = jnp.exp2(ext_scores - jnp.max(ext_scores, axis=-1, keepdims=True))
    ext_total = jnp.sum(ext_up, axis=-1, keepdims=True)
    gathered = [
        dot(up, vx[:CTX, lanes_of(side, at)]) for (side, head, at), up in zip(each, raised)
    ]
    spread = dot(ext_up.astype(BF16), vx[...]) * (1.0 / ext_total)
    for i, (side, head, at) in enumerate(each):
        acc = parts[side][6][part, at] * faded[i] + gathered[i]
        att_all[part, lanes_of(side, at)] = (acc / total[i]).astype(BF16)
    ext_att = jnp.concatenate(
        [
            spread[h * EXT : (h + 1) * EXT, h * HEAD_DIM : (h + 1) * HEAD_DIM]
            for h in range(2 * heads)
        ],
        axis=1,
    )
    tail = att_all.shape[0] - PAD
    att_all[tail:, :] = jnp.concatenate([ext_att, jnp.zeros_like(ext_att)], axis=0).astype(BF16)
    mix(att_all, frames, halo, wo, 1 - p, send)


def mix(att_all, frames, halo, wo, columns, out):
    p = lax.axis_index("mp")
    rows, width = frames.shape[0], out.shape[1]
    queries, tail = out.shape[0] - EXT, att_all.shape[0] - PAD
    here = pl.ds(pl.multiple_of(p * width, width), width)
    there = pl.ds(pl.multiple_of((1 - p) * width, width), width)
    lanes = pl.ds(pl.multiple_of(columns * width, width), width)
    projected = dot(att_all[:, :width], wo[here, :]) + dot(att_all[:, width:], wo[there, :])
    own = frames[rows_at(p * (rows - queries), queries), lanes].astype(F32)
    out[:queries] = (own + projected[:queries]).astype(BF16)
    edge = halo[rows_at(CTX * (1 - p), EXT), lanes].astype(F32)
    out[queries:] = (edge + projected[tail : tail + EXT]).astype(BF16)


def keep_kernel(att_all, frames, halo, wo, keep):
    mix(att_all, frames, halo, wo, lax.axis_index("mp"), keep)


def convolved(block, core, shift_by, weight, scale, shift, store):
    half = shift_by.shape[0] // KERNEL
    queries = block.shape[0] - EXT
    rows = rows_at(core * (queries - half), half)
    step = 256
    for at in range(0, block.shape[1], step):
        lanes = slice(at, at + step)
        gain = 0.5 * scale[:, lanes]
        u = jnp.broadcast_to(0.5 * shift[:, lanes], (half, step))
        for tap in range(KERNEL):
            moved = dot(shift_by[tap * half : (tap + 1) * half, :], block[:, lanes])
            u = u + moved * (weight[tap : tap + 1, lanes] * gain)
        plain = block[rows, lanes].astype(F32)
        store(lanes, (plain + (u + u * jnp.tanh(u))).astype(BF16))


def own_conv_kernel(keep, shift_by, weight, scale, shift, out):
    def store(lanes, value):
        out[:, lanes] = value

    convolved(keep, lax.axis_index("mp"), shift_by, weight, scale, shift, store)


def other_conv_kernel(got, done, shift_by, weight, scale, shift, out, block, sems):
    core = 1 - lax.axis_index("mp")
    half = done.shape[0]
    first = pltpu.make_async_copy(done, out.at[rows_at((1 - core) * half, half), :], sems.at[0])
    first.start()
    copies = [first]

    def store(lanes, value):
        block[:, lanes] = value
        copies.append(
            pltpu.make_async_copy(
                block.at[:, lanes], out.at[rows_at(core * half, half), lanes], sems.at[len(copies)]
            )
        )
        copies[-1].start()

    convolved(got, core, shift_by, weight, scale, shift, store)
    for copy in copies:
        copy.wait()


def call(kernel, out_shape, in_specs, out_specs, scratch=(), flops=0, size=0, exps=0, limit=16):
    return pl.pallas_call(
        kernel,
        out_shape=out_shape,
        in_specs=in_specs,
        out_specs=out_specs,
        scratch_shapes=scratch,
        compiler_params=pltpu.CompilerParams(vmem_limit_bytes=limit << 20),
        cost_estimate=pl.CostEstimate(flops=flops, bytes_accessed=size, transcendentals=exps),
    )


def compute(frames, valid, norm_gain, norm_bias, w_qkv, w_out, conv_weight, conv_scale, conv_shift):
    rows, model = frames.shape
    width = w_qkv.shape[2]
    heads = width // HEAD_DIM
    count = lax.axis_size("tm")
    half = rows // 2
    queries = half + EXT
    keys = half + EXT + CTX
    block = queries + EXT
    assert rows >= HALO + CTX and rows % 32 == 0
    shaped = jax.ShapeDtypeStruct
    pairs = []
    for i in range(count - 1):
        pairs += [(2 * i, 2 * (i + 1)), (2 * (i + 1) + 1, 2 * i + 1)]
    other = [(0, 1), (1, 0)]
    shift_shapes = (shaped((KERNEL * half, block), BF16),) * 2
    shifts = call(warm_kernel, shift_shapes, [], (VMEM,) * 2, flops=WARM_FLOPS)()
    sent = call(
        pick_kernel, shaped((HALO, model), BF16), [VMEM, ANY], VMEM, flops=PICK_FLOPS
    )(frames, shifts[0])
    halo = lax.ppermute(sent, ("tm", "mp"), pairs)
    w_other = lax.ppermute(w_qkv, "mp", other)
    wo_other = lax.ppermute(w_out, "mp", other)
    gain, bias = norm_gain.reshape(1, model), norm_bias.reshape(1, model)
    results = (
        shaped((queries, width), BF16),
        shaped((keys, width), BF16),
        shaped((keys, width), BF16),
        shaped((heads, queries, HEAD_DIM), F32),
        shaped((heads, queries, HEAD_DIM), F32),
        shaped((queries, width), F32),
        shaped((queries, width), BF16),
    )
    normed, count_here = call(
        norm_kernel,
        (shaped((keys, model), BF16), shaped((8, 256), jnp.int32)),
        [VMEM, SMEM, VMEM, VMEM],
        (VMEM,) * 2,
        flops=NORM_FLOPS,
        size=1_000_000,
    )(frames, valid, gain, bias)
    mine = call(
        first_kernel,
        results,
        [VMEM] * 3,
        (VMEM,) * 7,
        flops=1_300_000_000,
        size=4_000_000,
        exps=300_000,
    )(normed, w_qkv, count_here)
    second = call(
        second_kernel,
        results + shift_shapes,
        [VMEM] * 5,
        (VMEM,) * 9,
        flops=1_300_000_000,
        size=4_000_000,
        exps=300_000,
    )(normed, w_other, count_here, *shifts)
    theirs, (own_shift, other_shift) = second[:7], second[7:]
    send, att_all = call(
        halo_kernel,
        (shaped((block, width), BF16), shaped((pl.cdiv(queries, 16) * 16 + PAD, model), BF16)),
        [VMEM] * 21,
        (VMEM,) * 2,
        [
            pltpu.VMEM((HALO, model), BF16),
            pltpu.VMEM((SPAN, model), BF16),
            pltpu.VMEM((SPAN, model), BF16),
        ],
        flops=1_500_000_000,
        size=10_000_000,
        exps=300_000,
    )(halo, frames, gain, bias, wo_other, w_qkv, *mine, w_other, *theirs)
    got = lax.ppermute(send, "mp", other)
    keep = call(
        keep_kernel,
        shaped((block, width), BF16),
        [VMEM] * 4,
        VMEM,
        flops=200_000_000,
        size=1_000_000,
    )(att_all, frames, halo, w_out)
    weights = (conv_weight, conv_scale.reshape(1, width), conv_shift.reshape(1, width))
    done = call(
        own_conv_kernel,
        shaped((half, width), BF16),
        [VMEM] * 5,
        VMEM,
        flops=270_000_000,
        size=1_000_000,
    )(keep, own_shift, *weights)
    return call(
        other_conv_kernel,
        shaped((rows, width), BF16),
        [VMEM] * 6,
        ANY,
        [pltpu.VMEM((half, width), BF16), pltpu.SemaphoreType.DMA((1 + width // 256,))],
        flops=270_000_000,
        size=1_000_000,
    )(got, done, other_shift, *weights)


def solution(mesh):
    placed = (
        P("tm", None),
        P("tm"),
        P(),
        P(),
        P(None, None, "mp"),
        P(None, "mp"),
        P(None, "mp"),
        P("mp"),
        P("mp"),
    )
    return jax.shard_map(
        compute, mesh=mesh, in_specs=placed, out_specs=P("tm", "mp"), check_vma=False
    )
```

time: 21.5 us -> 18.6 us (0.87)
  Pallas kernels: 11.9 us -> 10.2 us
  local copies, waits for them, and re-layouts: 1.41 us -> 0.24 us
  waiting for transfers between devices: 2.31 us -> 2.06 us
  starting transfers between devices: 5.55 us -> 5.78 us
    pallas_call x6 -> x9, Pallas kernels: 11.9 us -> 10.2 us  [the longest x1 2.4 us: compute(): call(halo_kernel, (shaped((block, width), BF16), shaped((pl.cdiv(queries,...]
    unnamed x20 -> x18, local copies, waits for them, and re-layouts: 1.41 us -> 0.24 us
    ppermute x4, waiting for transfers between devices: 2.31 us -> 2.06 us  [the longest x1 1.66 us: compute(): halo = lax.ppermute(sent, ('tm', 'mp'), pairs)]
    ppermute x4, starting transfers between devices: 5.55 us -> 5.78 us  [the longest x1 5.15 us: compute(): halo = lax.ppermute(sent, ('tm', 'mp'), pairs)]
  transfers between devices with their start and end apart: 4 -> 4, of which waited for: 2 -> 2; matrix products, arithmetic and copies ran while one was open for 0% -> 0% of each run, Pallas kernels for 28% -> 36%
where the time goes in v3:
time: 18.6 us; the launch traced here: 18.4 us
  Pallas kernels  10.2 us (55%)
  starting transfers between devices  5.78 us (31%)
  waiting for transfers between devices  2.06 us (11%)
  local copies, waits for them, and re-layouts  0.24 us (1%)
    ppermute x1, starting transfers between devices, compute(): halo = lax.ppermute(sent, ('tm', 'mp'), pairs)  5.15 us
    pallas_call x1, Pallas kernels, compute(): call(halo_kernel, (shaped((block, width), BF16), shaped((pl.cdiv(queries,...  2.4 us
    pallas_call x1, Pallas kernels, compute(): call(second_kernel, results + shift_shapes, [VMEM] * 5, (VMEM,) * 9, flop...  2.18 us
    pallas_call x1, Pallas kernels, compute(): call(first_kernel, results, [VMEM] * 3, (VMEM,) * 7, flops=1300000000, si...  2.11 us
    ppermute x1, waiting for transfers between devices, compute(): halo = lax.ppermute(sent, ('tm', 'mp'), pairs)  1.66 us
    pallas_call x1, Pallas kernels, compute(): call(other_conv_kernel, shaped((rows, width), BF16), [VMEM] * 6, ANY, [pl...  1.22 us
    pallas_call x1, Pallas kernels, compute(): call(norm_kernel, (shaped((keys, model), BF16), shaped((8, 256), jnp.int3...  1 us
    pallas_call x1, Pallas kernels, compute(): call(own_conv_kernel, shaped((half, width), BF16), [VMEM] * 5, VMEM, flop...  0.56 us
  transfers between devices with their start and end apart: 4, of which 2 were waited for; matrix products, arithmetic and copies ran while one was open for 0% of the time, Pallas kernels for 36%

profile of v3, /device:TPU:0, one launch (start us, length us, event | category | flops | bytes accessed | tf_op | source)
XLA Modules:
  0.0 18.4 jit_solution(7382161141232064567)
XLA Ops:
  0.0 0.0 copy-start.1
  0.0 0.5 %collective-permute-start.2 = (bf16[3,1024,512]{2,1,0:T(8,128)(2,1)}, bf16[3,1024,512]{2,1,0:T(8,128)(2,1)S(1)}, u32[]{:S(2)}, u32[]{:S(2)}) collective-permute-start(bf16[3,1024,512]{2,1,0:T(8,128)(2,1)} %refs_0_.1), channel_id=1, source_target_pairs={{0,1},{1,0},{2,3},{3,2},{4,5},{5,4},{6,7},{7,6},{8,9},{9,8},{10,11... | collective-permute-start | bytes 9437192 | tf_op jit(solution)/shard_map/ppermute | solution.py:341
  0.5 0.1 collective-permute-start.1
  0.6 0.3 %shard_map.91 = (bf16[1440,176]{1,0:T(8,128)(2,1)S(1)}, bf16[1440,176]{1,0:T(8,128)(2,1)S(1)}) custom-call(), custom_call_target="tpu_custom_call" | custom-call | flops 1500000000 | tf_op jit(solution)/shard_map/pallas_call | solution.py:336
  0.9 0.0 copy-start.6
  0.9 0.0 copy-start.7
  0.9 0.0 copy-start.8
  0.9 0.2 %copy-done.1 = bf16[320,1024]{1,0:T(8,128)(2,1)S(1)} copy-done((bf16[320,1024]{1,0:T(8,128)(2,1)S(1)}, bf16[320,1024]{1,0:T(8,128)(2,1)}, u32[]{:S(2)}) %copy-start.1) | copy-done | bytes 655384
  1.1 0.0 copy-start
  1.1 5.2 %collective-permute-start = (bf16[136,1024]{1,0:T(8,128)(2,1)S(1)}, bf16[136,1024]{1,0:T(8,128)(2,1)S(1)}, u32[]{:S(2)}, u32[]{:S(2)}) collective-permute-start(bf16[136,1024]{1,0:T(8,128)(2,1)S(1)} %shard_map.92), channel_id=1, source_target_pairs={{0,2},{3,1},{2,4},{5,3},{4,6},{7,5},{6,8},{9,7},{8,10},{11,9},{10,... | collective-permute-start | bytes 835592 | tf_op jit(solution)/shard_map/ppermute | solution.py:340
  6.3 0.0 copy-done.6
  6.3 0.0 copy-done.7
  6.3 0.0 copy-done.8
  6.3 1.0 %shard_map.93 = (bf16[296,1024]{1,0:T(8,128)(2,1)S(1)}, s32[8,256]{1,0:T(8,128)S(1)}) custom-call(bf16[320,1024]{1,0:T(8,128)(2,1)S(1)} %copy-done.1, s32[320]{0:T(512)S(1)} %copy-done.8, f32[1,1024]{1,0:T(1,128)S(1)} %bitcast.8, f32[1,1024]{1,0:T(1,128)S(1)} %bitcast.10), custom_call_target="tpu_custom_call" | custom-call | flops 1500000000 | bytes 1000000 | tf_op jit(solution)/shard_map/pallas_call | solution.py:353
  7.3 0.0 copy-done
  7.3 2.1 %shard_map.94 = (bf16[168,512]{1,0:T(8,128)(2,1)S(1)}, bf16[296,512]{1,0:T(8,128)(2,1)S(1)}, bf16[296,512]{1,0:T(8,128)(2,1)S(1)}, f32[4,168,128]{2,1,0:T(8,128)...) custom-call(bf16[296,1024]{1,0:T(8,128)(2,1)S(1)} %get-tuple-element.28.normed, ...), custom_call_target="tpu_custom_call" | custom-call | flops 1300000000 | bytes 4000000 | tf_op jit(solution)/shard_map/pallas_call | solution.py:361
  9.4 0.0 collective-permute-done.2.w.refs_8_
  9.5 2.2 %shard_map.95 = (bf16[168,512]{1,0:T(8,128)(2,1)S(1)}, bf16[296,512]{1,0:T(8,128)(2,1)S(1)}, bf16[296,512]{1,0:T(8,128)(2,1)S(1)}, f32[4,168,128]{2,1,0:T(8,128)...) custom-call(bf16[296,1024]{1,0:T(8,128)(2,1)S(1)} %get-tuple-element, ...), custom_call_target="tpu_custom_call" | custom-call | flops 1300000000 | bytes 4000000 | tf_op jit(solution)/shard_map/pallas_call | solution.py:370
  11.6 1.7 %collective-permute-done.halo = bf16[136,1024]{1,0:T(8,128)(2,1)S(1)} collective-permute-done((bf16[136,1024]{1,0:T(8,128)(2,1)S(1)}, bf16[136,1024]{1,0:T(8,128)(2,1)S(1)}, u32[]{:S(2)}, u32[]{:S(2)}) %collective-permute-start) | collective-permute-done | bytes 278560 | tf_op jit(solution)/shard_map/ppermute | solution.py:340
  13.3 0.0 collective-permute-done.1.wo
  13.3 0.0 copy-start.2
  13.3 0.0 copy-start.3
  13.3 0.0 copy-start.4
  13.3 0.0 copy-start.5
  13.3 2.4 %shard_map.96 = (bf16[176,512]{1,0:T(8,128)(2,1)S(1)}, bf16[192,1024]{1,0:T(8,128)(2,1)S(1)}) custom-call(bf16[136,1024]{1,0:T(8,128)(2,1)S(1)} %collective-permute-done.halo, bf16[320,1024]{1,0:T(8,128)(2,1)S(1)} %copy-done.1, f32[1,1024]{1,0:T(1,128)S(1)} %bitcast.9, f32[1,1024]{1,0:T(1,128)S(1)} %bitcast.11, ...), custom_call_target="tpu_custom_call" | custom-call | flops 1500000000 | bytes 10000000 | tf_op jit(solution)/shard_map/pallas_call | solution.py:380
  15.7 0.1 collective-permute-start.3
  15.8 0.0 copy-done.2
  15.8 0.4 %shard_map.97.keep = bf16[176,512]{1,0:T(8,128)(2,1)S(1)} custom-call(bf16[192,1024]{1,0:T(8,128)(2,1)S(1)} %get-tuple-element.46.att_all, bf16[320,1024]{1,0:T(8,128)(2,1)S(1)} %copy-done.1, bf16[136,1024]{1,0:T(8,128)(2,1)S(1)} %collective-permute-done.halo, bf16[1024,512]{1,0:T(8,128)(2,1)S(1)} %copy-done.2), custom_call_target="tpu_custom_call" | custom-call | flops 200000000 | bytes 1000000 | tf_op jit(solution)/shard_map/pallas_call | solution.py:395
  16.2 0.0 copy-done.3
  16.2 0.0 copy-done.4
  16.2 0.0 copy-done.5
  16.3 0.6 %shard_map.98.done = bf16[160,512]{1,0:T(8,128)(2,1)S(1)} custom-call(bf16[176,512]{1,0:T(8,128)(2,1)S(1)} %shard_map.97.keep, bf16[1440,176]{1,0:T(8,128)(2,1)S(1)} %get-tuple-element.47.shift_by, f32[9,512]{1,0:T(8,128)S(1)} %copy-done.3, f32[1,512]{1,0:T(1,128)S(1)} %bitcast.4, f32[1,512]{1,0:T(1,128)S(1)} %bitcast.6), custom_call_target="tpu_custom_call" | custom-call | flops 270000000 | bytes 1000000 | tf_op jit(solution)/shard_map/pallas_call | solution.py:404
  16.8 0.4 %collective-permute-done.3.got = bf16[176,512]{1,0:T(8,128)(2,1)S(1)} collective-permute-done((bf16[176,512]{1,0:T(8,128)(2,1)S(1)}, bf16[176,512]{1,0:T(8,128)(2,1)S(1)}, u32[]{:S(2)}, u32[]{:S(2)}) %collective-permute-start.3) | collective-permute-done | bytes 180256 | tf_op jit(solution)/shard_map/ppermute | solution.py:394
  17.2 1.2 %shard_map.99 = bf16[320,512]{1,0:T(8,128)(2,1)} custom-call(bf16[176,512]{1,0:T(8,128)(2,1)S(1)} %collective-permute-done.3.got, bf16[160,512]{1,0:T(8,128)(2,1)S(1)} %shard_map.98.done, bf16[1440,176]{1,0:T(8,128)(2,1)S(1)} %get-tuple-element.48.shift_by, f32[9,512]{1,0:T(8,128)S(1)} %copy-done.3, f32[1,512]{1,0:T(1,128)S(1)} %bitcast.5, f32[1,512]{1,0:T(1,128)S(1)} %bitcast.7), custom_call_target="tpu_custom_call" | custom-call | flops 270000000 | bytes 1000000 | tf_op jit(solution)/shard_map/pallas_call | solution.py:412
  (1 shorter events, 0.0 us)
Async XLA Ops:
  0.0 1.1 %copy-start.1 = (bf16[320,1024]{1,0:T(8,128)(2,1)S(1)}, bf16[320,1024]{1,0:T(8,128)(2,1)}, u32[]{:S(2)}) copy-start(bf16[320,1024]{1,0:T(8,128)(2,1)} %frames.7) | copy-start | bytes 1966084
  0.0 9.4 %collective-permute-start.2 = (bf16[3,1024,512]{2,1,0:T(8,128)(2,1)}, bf16[3,1024,512]{2,1,0:T(8,128)(2,1)S(1)}, u32[]{:S(2)}, u32[]{:S(2)}) collective-permute-start(bf16[3,1024,512]{2,1,0:T(8,128)(2,1)} %refs_0_.1), channel_id=1, source_target_pairs={{0,1},{1,0},{2,3},{3,2},{4,5},{5,4},{6,7},{7,6},{8,9},{9,8},{10,11... | collective-permute-start | bytes 9437192 | tf_op jit(solution)/shard_map/ppermute | solution.py:341
  0.5 12.8 %collective-permute-start.1 = (bf16[1024,512]{1,0:T(8,128)(2,1)}, bf16[1024,512]{1,0:T(8,128)(2,1)S(1)}, u32[]{:S(2)}, u32[]{:S(2)}) collective-permute-start(bf16[1024,512]{1,0:T(8,128)(2,1)} %wo.1), channel_id=1, source_target_pairs={{0,1},{1,0},{2,3},{3,2},{4,5},{5,4},{6,7},{7,6},{8,9},{9,8},{10,11... | collective-permute-start | bytes 3145736 | tf_op jit(solution)/shard_map/ppermute | solution.py:342
  0.9 5.4 %copy-start.6 = (f32[1024]{0:T(1024)S(1)}, f32[1024]{0:T(1024)}, u32[]{:S(2)}) copy-start(f32[1024]{0:T(1024)} %param.11) | copy-start | bytes 12292
  0.9 5.4 %copy-start.7 = (f32[1024]{0:T(1024)S(1)}, f32[1024]{0:T(1024)}, u32[]{:S(2)}) copy-start(f32[1024]{0:T(1024)} %param.12) | copy-start | bytes 12292
  0.9 5.4 %copy-start.8 = (s32[320]{0:T(512)S(1)}, s32[320]{0:T(512)}, u32[]{:S(2)}) copy-start(s32[320]{0:T(512)} %valid.1) | copy-start | bytes 3844
  1.1 6.2 %copy-start = (bf16[3,1024,512]{2,1,0:T(8,128)(2,1)S(1)}, bf16[3,1024,512]{2,1,0:T(8,128)(2,1)}, u32[]{:S(2)}) copy-start(bf16[3,1024,512]{2,1,0:T(8,128)(2,1)} %refs_0_.1) | copy-start | bytes 9437188
  1.1 12.2 %collective-permute-start = (bf16[136,1024]{1,0:T(8,128)(2,1)S(1)}, bf16[136,1024]{1,0:T(8,128)(2,1)S(1)}, u32[]{:S(2)}, u32[]{:S(2)}) collective-permute-start(bf16[136,1024]{1,0:T(8,128)(2,1)S(1)} %shard_map.92), channel_id=1, source_target_pairs={{0,2},{3,1},{2,4},{5,3},{4,6},{7,5},{6,8},{9,7},{8,10},{11,9},{10,... | collective-permute-start | bytes 835592 | tf_op jit(solution)/shard_map/ppermute | solution.py:340
  13.3 2.5 %copy-start.2 = (bf16[1024,512]{1,0:T(8,128)(2,1)S(1)}, bf16[1024,512]{1,0:T(8,128)(2,1)}, u32[]{:S(2)}) copy-start(bf16[1024,512]{1,0:T(8,128)(2,1)} %wo.1) | copy-start | bytes 3145732
  13.3 2.9 %copy-start.3 = (f32[9,512]{1,0:T(8,128)S(1)}, f32[9,512]{1,0:T(8,128)}, u32[]{:S(2)}) copy-start(f32[9,512]{1,0:T(8,128)} %weight.3) | copy-start | bytes 55300
  13.3 2.9 %copy-start.4 = (f32[512]{0:T(512)S(1)}, f32[512]{0:T(512)}, u32[]{:S(2)}) copy-start(f32[512]{0:T(512)} %param.16) | copy-start | bytes 6148
  13.3 2.9 %copy-start.5 = (f32[512]{0:T(512)S(1)}, f32[512]{0:T(512)}, u32[]{:S(2)}) copy-start(f32[512]{0:T(512)} %param.17) | copy-start | bytes 6148
  15.7 1.5 %collective-permute-start.3 = (bf16[176,512]{1,0:T(8,128)(2,1)S(1)}, bf16[176,512]{1,0:T(8,128)(2,1)S(1)}, u32[]{:S(2)}, u32[]{:S(2)}) collective-permute-start(bf16[176,512]{1,0:T(8,128)(2,1)S(1)} %get-tuple-element.45), channel_id=1, source_target_pairs={{0,1},{1,0},{2,3},{3,2},{4,5},{5,4},{6,7},{7,6},{8,9},{9,8},{10,11... | collective-permute-start | bytes 540680 | tf_op jit(solution)/shard_map/ppermute | solution.py:394
